TPU v7x, 32 devices: a whole 2x2x4 slice. The times are simulated.
32 devices in a mesh: section: 8 (over z, core), ctx: 4 (over y, x).
Axes of the slice: x: 2, y: 2, z: 4, core: 2. Of those that a mesh axis runs over, the one named last changes fastest.
Arguments:
- queries: bfloat16 [8, 2, 512, 4096], P('section', None, 'ctx'), may hold values from -6 to 6
- keyvals: bfloat16 [8, 2, 2, 512, 512], P('section', None, None, 'ctx'), may hold values from -6 to 6
- saved_out: bfloat16 [8, 2, 512, 4096], P('section', None, 'ctx'), may hold values from -4 to 4
- grad_in: bfloat16 [8, 512, 4096], P('section', 'ctx'), may hold values from -6 to 6
- section_layers: int32 [8], replicated, may hold values from 1 to 2, as said below
- span_order: int32 [8], replicated, may hold values from 0 to 7, as said below
Outputs:
- grad_kv: bfloat16 [8, 2, 2, 512, 512], P('section', None, None, 'ctx')
- grad_down: bfloat16 [8, 512, 4096], P('section', 'ctx')
Inputs may be any that keep to these rules, and one draw needn't show every extreme that they name: `section_layers`: some section owns 2 layers and some section owns 1. `span_order`: A permutation; entries 2 c and 2 c + 1 sum to 7.
All inputs are finite; a program needn't handle non-finite values.
Results may differ from a plain program's by a relative error of at most 0.0074.
Values may be sent and summed in bfloat16 or wider, within the bound.
No kernel may reach another device: no remote copies, remote signals or barrier semaphores. Data moves between devices by JAX's collectives and lax.ppermute only.
A program may use at most 128 MiB of HBM per device.

v0:
```python
import jax
import jax.numpy as jnp
from jax import lax
from jax.sharding import PartitionSpec as P

DH = 128


def shifted(array, axis, by):
    length = lax.axis_size(axis)
    return lax.ppermute(array, axis, [(i, (i + by) % length) for i in range(length)])


def span_pair(order_rows, device):
    picked = (jnp.arange(order_rows.shape[0]) == device)[:, None]
    return jnp.sum(jnp.where(picked, order_rows, 0), axis=0)


def on_device(queries, keyvals, saved_out, grad_in, section_layers, span_order):
    cycle_size = lax.axis_size("ctx")
    own_index = lax.axis_index("ctx")
    section_index = lax.axis_index("section")
    slots = queries.shape[1]
    tokens = queries.shape[2]
    width = queries.shape[3]
    kv_width = keyvals.shape[4]
    groups = kv_width // DH
    repeat = width // kv_width
    span_rows = tokens // 2
    score_scale = DH ** (-0.5)
    layer_count = jnp.sum(
        jnp.where(jnp.arange(section_layers.shape[0]) == section_index, section_layers, 0)
    )
    order_rows = span_order.reshape(cycle_size, 2)
    own_spans = span_pair(order_rows, own_index)
    offsets = jnp.arange(span_rows, dtype=jnp.int32)

    def block_visible(query_span, key_span):
        return (key_span * span_rows + offsets)[None, :] <= (query_span * span_rows + offsets)[
            :, None
        ]

    def stats_shard(running, key_shard, key_spans, query_heads, enabled):
        maxima, totals = running
        new_maxima = []
        new_totals = []
        for query_part in range(2):
            state = (maxima[query_part], totals[query_part])
            query_span = query_heads[query_part * span_rows : (query_part + 1) * span_rows]
            for key_part in range(2):
                key_span = key_shard[key_part * span_rows : (key_part + 1) * span_rows].reshape(
                    span_rows, groups, DH
                )

                def stats_visit(
                    inner_state,
                    query_span=query_span,
                    key_span=key_span,
                    query_part=query_part,
                    key_part=key_part,
                ):
                    old_max, old_total = inner_state
                    scores = (
                        jnp.einsum(
                            "qgrd,kgd->grqk",
                            query_span,
                            key_span,
                            preferred_element_type=jnp.float32,
                        )
                        * score_scale
                    )
                    visible = block_visible(own_spans[query_part], key_spans[key_part])
                    scores = jnp.where(visible, scores, -1e30)
                    new_max = jnp.maximum(old_max, jnp.max(scores, axis=-1))
                    added = jnp.sum(
                        jnp.where(visible, jnp.exp(scores - new_max[..., None]), 0.0), axis=-1
                    )
                    return (new_max, old_total * jnp.exp(old_max - new_max) + added)

                wanted = jnp.logical_and(enabled, key_spans[key_part] <= own_spans[query_part])
                state = lax.cond(wanted, stats_visit, lambda inner_state: inner_state, state)
            new_maxima.append(state[0])
            new_totals.append(state[1])
        return (jnp.stack(new_maxima), jnp.stack(new_totals))

    def gradient_shard(
        key_block, key_spans, query_heads, grad_heads, row_dots, log_totals, enabled
    ):
        zero_query = jnp.zeros((span_rows, groups, repeat, DH), jnp.float32)
        zero_key = jnp.zeros((span_rows, groups, DH), jnp.float32)
        query_grads = [zero_query, zero_query]
        key_grads = [zero_key, zero_key]
        value_grads = [zero_key, zero_key]
        for query_part in range(2):
            query_span = query_heads[query_part * span_rows : (query_part + 1) * span_rows]
            grad_span = grad_heads[query_part * span_rows : (query_part + 1) * span_rows]
            for key_part in range(2):
                key_span = key_block[0, key_part * span_rows : (key_part + 1) * span_rows].reshape(
                    span_rows, groups, DH
                )
                value_span = key_block[
                    1, key_part * span_rows : (key_part + 1) * span_rows
                ].reshape(span_rows, groups, DH)

                def gradient_visit(
                    unused,
                    query_span=query_span,
                    grad_span=grad_span,
                    key_span=key_span,
                    value_span=value_span,
                    query_part=query_part,
                    key_part=key_part,
                ):
                    scores = (
                        jnp.einsum(
                            "qgrd,kgd->grqk",
                            query_span,
                            key_span,
                            preferred_element_type=jnp.float32,
                        )
                        * score_scale
                    )
                    visible = block_visible(own_spans[query_part], key_spans[key_part])
                    probs = jnp.where(
                        visible, jnp.exp(scores - log_totals[query_part][..., None]), 0.0
                    ).astype(jnp.bfloat16)
                    grad_probs = jnp.einsum(
                        "qgrd,kgd->grqk", grad_span, value_span, preferred_element_type=jnp.float32
                    )
                    grad_scores = (
                        probs.astype(jnp.float32) * (grad_probs - row_dots[query_part][..., None])
                    ).astype(jnp.bfloat16)
                    value_grad = jnp.einsum(
                        "grqk,qgrd->kgd", probs, grad_span, preferred_element_type=jnp.float32
                    )
                    key_grad = (
                        jnp.einsum(
                            "grqk,qgrd->kgd",
                            grad_scores,
                            query_span,
                            preferred_element_type=jnp.float32,
                        )
                        * score_scale
                    )
                    query_grad = (
                        jnp.einsum(
                            "grqk,kgd->qgrd",
                            grad_scores,
                            key_span,
                            preferred_element_type=jnp.float32,
                        )
                        * score_scale
                    )
                    return (query_grad, key_grad, value_grad)

                def hidden_pair(unused):
                    return (zero_query, zero_key, zero_key)

                wanted = jnp.logical_and(enabled, key_spans[key_part] <= own_spans[query_part])
                query_grad, key_grad, value_grad = lax.cond(wanted, gradient_visit, hidden_pair, 0)
                query_grads[query_part] = query_grads[query_part] + query_grad
                key_grads[key_part] = key_grads[key_part] + key_grad
                value_grads[key_part] = value_grads[key_part] + value_grad
        query_total = jnp.concatenate(query_grads, axis=0)
        key_total = jnp.stack(
            [jnp.concatenate(key_grads, axis=0), jnp.concatenate(value_grads, axis=0)]
        ).reshape(2, tokens, kv_width)
        return (query_total, key_total)

    gradient = grad_in[0]
    results = [None] * slots
    for slot in reversed(range(slots)):
        live = slot < layer_count
        enabled = True
        key_values = keyvals[0, slot]
        layer_query_heads = queries[0, slot].reshape(tokens, groups, repeat, DH)
        layer_grad_heads = gradient.reshape(tokens, groups, repeat, DH)
        out_heads = saved_out[0, slot].reshape(tokens, groups, repeat, DH)
        layer_row_dots = jnp.sum(
            layer_grad_heads.astype(jnp.float32) * out_heads.astype(jnp.float32), axis=-1
        )
        layer_row_dots = layer_row_dots.reshape(2, span_rows, groups, repeat).transpose(0, 2, 3, 1)
        initial = (
            jnp.full((2, groups, repeat, span_rows), -1e30, jnp.float32),
            jnp.zeros((2, groups, repeat, span_rows), jnp.float32),
        )
        key_piece = lax.all_gather(key_values[0], "ctx", axis=0, tiled=True)

        def piece_step(shard_index, inner_state):
            key_shard = lax.dynamic_slice_in_dim(key_piece, shard_index * tokens, tokens, 0)
            return stats_shard(
                inner_state,
                key_shard,
                span_pair(order_rows, shard_index),
                layer_query_heads,
                enabled,
            )

        layer_maxima, layer_totals = lax.fori_loop(
            0, key_piece.shape[0] // tokens, piece_step, initial
        )
        layer_log_totals = layer_maxima + jnp.log(layer_totals)

        def cycle_step(step_index, running):
            travel_block, travel_grads, query_acc = running
            source = (own_index - step_index) % cycle_size
            query_part_grad, key_part_grad = gradient_shard(
                travel_block,
                span_pair(order_rows, source),
                layer_query_heads,
                layer_grad_heads,
                layer_row_dots,
                layer_log_totals,
                enabled,
            )
            travel_grads = travel_grads + key_part_grad
            travel_block = shifted(travel_block, "ctx", 1)
            travel_grads = shifted(travel_grads, "ctx", 1)
            return (travel_block, travel_grads, query_acc + query_part_grad)

        unused_block, key_value_grad, layer_query_grad = lax.fori_loop(
            0,
            cycle_size,
            cycle_step,
            (
                key_values,
                jnp.zeros((2, tokens, kv_width), jnp.float32),
                jnp.zeros((tokens, groups, repeat, DH), jnp.float32),
            ),
        )
        new_gradient = (
            gradient.astype(jnp.float32) + layer_query_grad.reshape(tokens, width)
        ).astype(jnp.bfloat16)
        new_gradient, key_value_grad = (new_gradient, key_value_grad.astype(jnp.bfloat16))
        gradient = jnp.where(live, new_gradient, gradient)
        key_value_grad = jnp.where(live, key_value_grad, jnp.zeros_like(key_value_grad))
        results[slot] = key_value_grad
    grad_kv = jnp.stack(results)[None]
    grad_down = shifted(gradient[None], "section", -1)
    return (grad_kv, grad_down)


def solution(mesh):
    in_specs = (
        P("section", None, "ctx", None),
        P("section", None, None, "ctx", None),
        P("section", None, "ctx", None),
        P("section", "ctx", None),
        P(),
        P(),
    )
    out_specs = (P("section", None, None, "ctx", None), P("section", "ctx", None))
    return jax.shard_map(
        on_device, mesh=mesh, in_specs=in_specs, out_specs=out_specs, check_vma=False
    )
```

profile of v0, /device:TPU:13, one launch (start us, length us, event | category | flops | bytes accessed | tf_op | source)
XLA Modules:
  0.0 629.9 jit_solution(3862780603305160126)
XLA Ops:
  9.1 8.6 %all-gather = bf16[1,1,1,512,512]{4,3,2,1,0:T(8,128)(2,1)} all-gather(bf16[1,1,1,128,512]{4,3,2,1,0:T(8,128)(2,1)S(1)} %get-tuple-element.2229), channel_id=2, replica_groups=mesh['section'=8,'ctx'=4] {'ctx'}, dimensions={3}, use_global_device_ids=true | all-gather | bytes 655360 | tf_op jit(solution)/shard_map/all_gather | solution.py:187
  17.8 80.4 %while.76 = (s32[]{:T(128)}, f32[2,4,8,64]{3,2,1,0:T(8,128)S(1)}, f32[2,4,8,64]{3,2,1,0:T(8,128)S(1)}, s32[4,2]{0,1:T(2,128)S(1)}, s32[2]{0:T(128)S(1)}, /*index...) while((s32[]{:T(128)}, f32[2,4,8,64]{3,2,1,0:T(8,128)S(1)}, ...), condition=%wide.region_20.21_spmd.clone.clone, body=%wide.region_2.20_spmd.clone.clone.sunk | while | flops 137404960 | bytes 9788499 | solution.py:199
  24.7 4.2 conditional.64
  30.9 5.5 conditional.65
  42.8 4.4 conditional.67
  50.3 5.5 conditional.65
  66.5 4.2 conditional.64
  72.7 5.5 conditional.65
  85.7 4.2 conditional.64
  92.0 5.5 conditional.65
  108.0 198.6 %while.78 = (s32[]{:T(128)}, bf16[2,128,512]{2,1,0:T(8,128)(2,1)}, f32[2,128,512]{2,1,0:T(8,128)}, f32[128,4,8,128]{3,0,2,1:T(8,128)}, s32[]{:T(128)}, /*index=5...) while((s32[]{:T(128)}, bf16[2,128,512]{2,1,0:T(8,128)(2,1)}, ...), condition=%wide.region_32.33_spmd.clone.clone, body=%wide.region_22.32_spmd.clone.clone.sunk | while | flops 679100928 | bytes 74817304 | solution.py:221
  122.7 4.8 conditional.74
  129.2 5.5 conditional.73
  149.7 12.6 %collective-permute-done = bf16[2,128,512]{2,1,0:T(8,128)(2,1)} collective-permute-done((bf16[2,128,512]{2,1,0:T(8,128)(2,1)S(1)}, bf16[2,128,512]{2,1,0:T(8,128)(2,1)}, u32[]{:S(2)}, u32[]{:S(2)}) %collective-permute-start) | collective-permute-done | bytes 262176 | tf_op jit(solution)/shard_map/while/body/eval_jaxpr/ppermute | solution.py:11
  175.6 5.5 conditional.73
  182.2 5.9 conditional.72
  202.0 9.8 %collective-permute-done = bf16[2,128,512]{2,1,0:T(8,128)(2,1)} collective-permute-done((bf16[2,128,512]{2,1,0:T(8,128)(2,1)S(1)}, bf16[2,128,512]{2,1,0:T(8,128)(2,1)}, u32[]{:S(2)}, u32[]{:S(2)}) %collective-permute-start) | collective-permute-done | bytes 262176 | tf_op jit(solution)/shard_map/while/body/eval_jaxpr/ppermute | solution.py:11
  228.5 5.5 conditional.73
  250.4 9.3 %collective-permute-done = bf16[2,128,512]{2,1,0:T(8,128)(2,1)} collective-permute-done((bf16[2,128,512]{2,1,0:T(8,128)(2,1)S(1)}, bf16[2,128,512]{2,1,0:T(8,128)(2,1)}, u32[]{:S(2)}, u32[]{:S(2)}) %collective-permute-start) | collective-permute-done | bytes 262176 | tf_op jit(solution)/shard_map/while/body/eval_jaxpr/ppermute | solution.py:11
  276.3 5.5 conditional.73
  299.3 7.3 %collective-permute-done = bf16[2,128,512]{2,1,0:T(8,128)(2,1)} collective-permute-done((bf16[2,128,512]{2,1,0:T(8,128)(2,1)S(1)}, bf16[2,128,512]{2,1,0:T(8,128)(2,1)}, u32[]{:S(2)}, u32[]{:S(2)}) %collective-permute-start) | collective-permute-done | bytes 262176 | tf_op jit(solution)/shard_map/while/body/eval_jaxpr/ppermute | solution.py:11
  308.5 4.2 copy.80
  324.3 7.3 %all-gather.1 = bf16[1,1,1,512,512]{4,3,2,1,0:T(8,128)(2,1)S(1)} all-gather(bf16[1,1,1,128,512]{4,3,2,1,0:T(8,128)(2,1)S(1)} %copy-done.42), channel_id=3, replica_groups=mesh['section'=8,'ctx'=4] {'ctx'}, dimensions={3}, use_global_device_ids=true | all-gather | bytes 655360 | tf_op jit(solution)/shard_map/all_gather | solution.py:187
  331.6 75.5 %while.77 = (s32[]{:T(128)}, f32[2,4,8,64]{3,2,1,0:T(8,128)S(1)}, f32[2,4,8,64]{3,2,1,0:T(8,128)S(1)}, s32[4,2]{0,1:T(2,128)S(1)}, s32[2]{0:T(128)S(1)}, /*index...) while((s32[]{:T(128)}, f32[2,4,8,64]{3,2,1,0:T(8,128)S(1)}, ...), condition=%wide.region_51.52_spmd.clone.clone, body=%wide.region_33.51_spmd.clone.clone.sunk | while | flops 137404960 | bytes 9788499 | solution.py:199
  337.5 4.3 conditional.68
  343.7 5.3 conditional.69
  354.4 4.2 conditional.71
  361.7 5.3 conditional.69
  376.7 4.3 conditional.68
  382.9 5.3 conditional.69
  394.8 4.3 conditional.68
  401.0 5.3 conditional.69
  408.6 182.7 %while.79 = (s32[]{:T(128)}, bf16[2,128,512]{2,1,0:T(8,128)(2,1)}, f32[2,128,512]{2,1,0:T(8,128)}, f32[128,4,8,128]{3,0,2,1:T(8,128)}, s32[]{:T(128)}, /*index=5...) while((s32[]{:T(128)}, bf16[2,128,512]{2,1,0:T(8,128)(2,1)}, ...), condition=%wide.region_63.64_spmd.clone.clone, body=%wide.region_53.63_spmd.clone.clone.sunk | while | flops 679100928 | bytes 74817304 | solution.py:221
  423.4 4.8 conditional.78
  430.0 5.5 conditional.77
  450.4 7.2 %collective-permute-done.2 = bf16[2,128,512]{2,1,0:T(8,128)(2,1)} collective-permute-done((bf16[2,128,512]{2,1,0:T(8,128)(2,1)S(1)}, bf16[2,128,512]{2,1,0:T(8,128)(2,1)}, u32[]{:S(2)}, u32[]{:S(2)}) %collective-permute-start.2) | collective-permute-done | bytes 262176 | tf_op jit(solution)/shard_map/while/body/eval_jaxpr/ppermute | solution.py:11
  470.9 5.5 conditional.77
  477.5 5.9 conditional.76
  497.0 5.6 collective-permute-done.2
  512.7 3.6 conditional.79
  519.4 5.5 conditional.77
  540.9 6.0 collective-permute-done.2
  557.0 3.6 conditional.79
  563.7 5.5 conditional.77
  585.7 5.6 collective-permute-done.2
  591.3 4.2 copy.81
  602.5 12.8 %collective-permute-start.4 = (bf16[1,128,4096]{2,1,0:T(8,128)(2,1)S(1)}, bf16[1,128,4096]{2,1,0:T(8,128)(2,1)S(1)}, u32[]{:S(2)}, u32[]{:S(2)}) collective-permute-start(bf16[1,128,4096]{2,1,0:T(8,128)(2,1)S(1)} %fusion.148), channel_id=1, source_target_pairs={{0,28},{4,0},{8,4},{12,8},{16,12},{20,16},{24,20},{28,24},{1,29},{... | collective-permute-start | bytes 3145736 | tf_op jit(solution)/shard_map/ppermute | solution.py:11
  617.4 11.6 %collective-permute-done.4 = bf16[1,128,4096]{2,1,0:T(8,128)(2,1)S(1)} collective-permute-done((bf16[1,128,4096]{2,1,0:T(8,128)(2,1)S(1)}, bf16[1,128,4096]{2,1,0:T(8,128)(2,1)S(1)}, u32[]{:S(2)}, u32[]{:S(2)}) %collective-permute-start.4) | collective-permute-done | bytes 1048608 | tf_op jit(solution)/shard_map/ppermute | solution.py:11
  (1053 shorter events, 435.9 us)
Async XLA Ops:
  17.8 80.4 %copy-start.35 = (bf16[1,128,4096]{2,1,0:T(8,128)(2,1)S(1)}, bf16[1,128,4096]{2,1,0:T(8,128)(2,1)}, u32[]{:S(2)}) copy-start(bf16[1,128,4096]{2,1,0:T(8,128)(2,1)} %param.49) | copy-start | bytes 3145732
  98.9 6.5 %copy-start.10 = (bf16[1,128,4096]{1,2,0:T(8,128)(2,1)}, bf16[1,128,4096]{1,2,0:T(8,128)(2,1)S(1)}, u32[]{:S(2)}) copy-start(bf16[1,128,4096]{1,2,0:T(8,128)(2,1)S(1)} %copy.63) | copy-start | bytes 3145732
  111.6 6.5 %copy-start.12 = (bf16[64,4,128]{2,1,0:T(4,128)(2,1)S(1)}, bf16[64,4,128]{2,1,0:T(4,128)(2,1)}, u32[]{:S(2)}) copy-start(bf16[64,4,128]{2,1,0:T(4,128)(2,1)} %squeeze.374) | copy-start | bytes 196612 | tf_op jit(solution)/shard_map/while
  111.6 6.5 %copy-start.16 = (bf16[64,4,128]{2,1,0:T(4,128)(2,1)S(1)}, bf16[64,4,128]{2,1,0:T(4,128)(2,1)}, u32[]{:S(2)}) copy-start(bf16[64,4,128]{2,1,0:T(4,128)(2,1)} %squeeze.375) | copy-start | bytes 196612 | tf_op jit(solution)/shard_map/while
  111.6 6.5 %copy-start.40 = (f32[2,4,8,64]{3,2,1,0:T(8,128)S(1)}, f32[2,4,8,64]{3,2,1,0:T(8,128)}, u32[]{:S(2)}) copy-start(f32[2,4,8,64]{3,2,1,0:T(8,128)} %get-tuple-element.2786) | copy-start | bytes 49156 | tf_op jit(solution)/shard_map/while
  111.6 6.5 %copy-start.41 = (f32[2,4,8,64]{3,2,1,0:T(8,128)S(1)}, f32[2,4,8,64]{3,2,1,0:T(8,128)}, u32[]{:S(2)}) copy-start(f32[2,4,8,64]{3,2,1,0:T(8,128)} %get-tuple-element.2785) | copy-start | bytes 49156 | tf_op jit(solution)/shard_map/while
  144.7 17.6 %collective-permute-start.1 = (f32[2,128,512]{2,1,0:T(8,128)}, f32[2,128,512]{2,1,0:T(8,128)}, u32[]{:S(2)}, u32[]{:S(2)}) collective-permute-start(f32[2,128,512]{2,1,0:T(8,128)} %maximum_add_fusion.8), channel_id=1, source_target_pairs={{0,1},{1,2},{2,3},{3,0},{4,5},{5,6},{6,7},{7,4},{8,9},{9,10},{10,1... | collective-permute-start | bytes 1572872 | tf_op jit(solution)/shard_map/while/body/eval_jaxpr/ppermute | solution.py:11
  144.7 17.5 %collective-permute-start = (bf16[2,128,512]{2,1,0:T(8,128)(2,1)S(1)}, bf16[2,128,512]{2,1,0:T(8,128)(2,1)}, u32[]{:S(2)}, u32[]{:S(2)}) collective-permute-start(bf16[2,128,512]{2,1,0:T(8,128)(2,1)S(1)} %copy.364), channel_id=1, source_target_pairs={{0,1},{1,2},{2,3},{3,0},{4,5},{5,6},{6,7},{7,4},{8,9},{9,10},{10,1... | collective-permute-start | bytes 786440 | tf_op jit(solution)/shard_map/while/body/eval_jaxpr/ppermute | solution.py:11
  165.9 6.5 %copy-start.12 = (bf16[64,4,128]{2,1,0:T(4,128)(2,1)S(1)}, bf16[64,4,128]{2,1,0:T(4,128)(2,1)}, u32[]{:S(2)}) copy-start(bf16[64,4,128]{2,1,0:T(4,128)(2,1)} %squeeze.374) | copy-start | bytes 196612 | tf_op jit(solution)/shard_map/while
  165.9 6.5 %copy-start.16 = (bf16[64,4,128]{2,1,0:T(4,128)(2,1)S(1)}, bf16[64,4,128]{2,1,0:T(4,128)(2,1)}, u32[]{:S(2)}) copy-start(bf16[64,4,128]{2,1,0:T(4,128)(2,1)} %squeeze.375) | copy-start | bytes 196612 | tf_op jit(solution)/shard_map/while
  165.9 6.5 %copy-start.40 = (f32[2,4,8,64]{3,2,1,0:T(8,128)S(1)}, f32[2,4,8,64]{3,2,1,0:T(8,128)}, u32[]{:S(2)}) copy-start(f32[2,4,8,64]{3,2,1,0:T(8,128)} %get-tuple-element.2786) | copy-start | bytes 49156 | tf_op jit(solution)/shard_map/while
  165.9 6.5 %copy-start.41 = (f32[2,4,8,64]{3,2,1,0:T(8,128)S(1)}, f32[2,4,8,64]{3,2,1,0:T(8,128)}, u32[]{:S(2)}) copy-start(f32[2,4,8,64]{3,2,1,0:T(8,128)} %get-tuple-element.2785) | copy-start | bytes 49156 | tf_op jit(solution)/shard_map/while
  181.1 9.9 %copy-start.20 = (f32[64,4,128]{2,0,1:T(8,128)S(1)}, f32[64,4,128]{2,0,1:T(8,128)}, u32[]{:S(2)}) copy-start(f32[64,4,128]{2,0,1:T(8,128)} %copy-done.19) | copy-start | bytes 393220 | tf_op jit(solution)/shard_map/while
  181.1 9.9 %copy-start.22 = (f32[64,4,128]{2,0,1:T(8,128)S(1)}, f32[64,4,128]{2,0,1:T(8,128)}, u32[]{:S(2)}) copy-start(f32[64,4,128]{2,0,1:T(8,128)} %copy-done.21) | copy-start | bytes 393220 | tf_op jit(solution)/shard_map/while
  195.2 16.6 %collective-permute-start.1 = (f32[2,128,512]{2,1,0:T(8,128)}, f32[2,128,512]{2,1,0:T(8,128)}, u32[]{:S(2)}, u32[]{:S(2)}) collective-permute-start(f32[2,128,512]{2,1,0:T(8,128)} %maximum_add_fusion.8), channel_id=1, source_target_pairs={{0,1},{1,2},{2,3},{3,0},{4,5},{5,6},{6,7},{7,4},{8,9},{9,10},{10,1... | collective-permute-start | bytes 1572872 | tf_op jit(solution)/shard_map/while/body/eval_jaxpr/ppermute | solution.py:11
  195.2 16.6 %collective-permute-start = (bf16[2,128,512]{2,1,0:T(8,128)(2,1)S(1)}, bf16[2,128,512]{2,1,0:T(8,128)(2,1)}, u32[]{:S(2)}, u32[]{:S(2)}) collective-permute-start(bf16[2,128,512]{2,1,0:T(8,128)(2,1)S(1)} %copy.364), channel_id=1, source_target_pairs={{0,1},{1,2},{2,3},{3,0},{4,5},{5,6},{6,7},{7,4},{8,9},{9,10},{10,1... | collective-permute-start | bytes 786440 | tf_op jit(solution)/shard_map/while/body/eval_jaxpr/ppermute | solution.py:11
  215.4 6.5 %copy-start.12 = (bf16[64,4,128]{2,1,0:T(4,128)(2,1)S(1)}, bf16[64,4,128]{2,1,0:T(4,128)(2,1)}, u32[]{:S(2)}) copy-start(bf16[64,4,128]{2,1,0:T(4,128)(2,1)} %squeeze.374) | copy-start | bytes 196612 | tf_op jit(solution)/shard_map/while
  215.5 6.5 %copy-start.16 = (bf16[64,4,128]{2,1,0:T(4,128)(2,1)S(1)}, bf16[64,4,128]{2,1,0:T(4,128)(2,1)}, u32[]{:S(2)}) copy-start(bf16[64,4,128]{2,1,0:T(4,128)(2,1)} %squeeze.375) | copy-start | bytes 196612 | tf_op jit(solution)/shard_map/while
  215.5 6.5 %copy-start.40 = (f32[2,4,8,64]{3,2,1,0:T(8,128)S(1)}, f32[2,4,8,64]{3,2,1,0:T(8,128)}, u32[]{:S(2)}) copy-start(f32[2,4,8,64]{3,2,1,0:T(8,128)} %get-tuple-element.2786) | copy-start | bytes 49156 | tf_op jit(solution)/shard_map/while
  215.5 6.5 %copy-start.41 = (f32[2,4,8,64]{3,2,1,0:T(8,128)S(1)}, f32[2,4,8,64]{3,2,1,0:T(8,128)}, u32[]{:S(2)}) copy-start(f32[2,4,8,64]{3,2,1,0:T(8,128)} %get-tuple-element.2785) | copy-start | bytes 49156 | tf_op jit(solution)/shard_map/while
  244.0 15.7 %collective-permute-start.1 = (f32[2,128,512]{2,1,0:T(8,128)}, f32[2,128,512]{2,1,0:T(8,128)}, u32[]{:S(2)}, u32[]{:S(2)}) collective-permute-start(f32[2,128,512]{2,1,0:T(8,128)} %maximum_add_fusion.8), channel_id=1, source_target_pairs={{0,1},{1,2},{2,3},{3,0},{4,5},{5,6},{6,7},{7,4},{8,9},{9,10},{10,1... | collective-permute-start | bytes 1572872 | tf_op jit(solution)/shard_map/while/body/eval_jaxpr/ppermute | solution.py:11
  244.1 15.5 %collective-permute-start = (bf16[2,128,512]{2,1,0:T(8,128)(2,1)S(1)}, bf16[2,128,512]{2,1,0:T(8,128)(2,1)}, u32[]{:S(2)}, u32[]{:S(2)}) collective-permute-start(bf16[2,128,512]{2,1,0:T(8,128)(2,1)S(1)} %copy.364), channel_id=1, source_target_pairs={{0,1},{1,2},{2,3},{3,0},{4,5},{5,6},{6,7},{7,4},{8,9},{9,10},{10,1... | collective-permute-start | bytes 786440 | tf_op jit(solution)/shard_map/while/body/eval_jaxpr/ppermute | solution.py:11
  263.3 6.5 %copy-start.12 = (bf16[64,4,128]{2,1,0:T(4,128)(2,1)S(1)}, bf16[64,4,128]{2,1,0:T(4,128)(2,1)}, u32[]{:S(2)}) copy-start(bf16[64,4,128]{2,1,0:T(4,128)(2,1)} %squeeze.374) | copy-start | bytes 196612 | tf_op jit(solution)/shard_map/while
  263.3 6.5 %copy-start.16 = (bf16[64,4,128]{2,1,0:T(4,128)(2,1)S(1)}, bf16[64,4,128]{2,1,0:T(4,128)(2,1)}, u32[]{:S(2)}) copy-start(bf16[64,4,128]{2,1,0:T(4,128)(2,1)} %squeeze.375) | copy-start | bytes 196612 | tf_op jit(solution)/shard_map/while
  263.3 6.5 %copy-start.40 = (f32[2,4,8,64]{3,2,1,0:T(8,128)S(1)}, f32[2,4,8,64]{3,2,1,0:T(8,128)}, u32[]{:S(2)}) copy-start(f32[2,4,8,64]{3,2,1,0:T(8,128)} %get-tuple-element.2786) | copy-start | bytes 49156 | tf_op jit(solution)/shard_map/while
  263.3 6.5 %copy-start.41 = (f32[2,4,8,64]{3,2,1,0:T(8,128)S(1)}, f32[2,4,8,64]{3,2,1,0:T(8,128)}, u32[]{:S(2)}) copy-start(f32[2,4,8,64]{3,2,1,0:T(8,128)} %get-tuple-element.2785) | copy-start | bytes 49156 | tf_op jit(solution)/shard_map/while
  291.8 14.8 %collective-permute-start.1 = (f32[2,128,512]{2,1,0:T(8,128)}, f32[2,128,512]{2,1,0:T(8,128)}, u32[]{:S(2)}, u32[]{:S(2)}) collective-permute-start(f32[2,128,512]{2,1,0:T(8,128)} %maximum_add_fusion.8), channel_id=1, source_target_pairs={{0,1},{1,2},{2,3},{3,0},{4,5},{5,6},{6,7},{7,4},{8,9},{9,10},{10,1... | collective-permute-start | bytes 1572872 | tf_op jit(solution)/shard_map/while/body/eval_jaxpr/ppermute | solution.py:11
  291.8 14.8 %collective-permute-start = (bf16[2,128,512]{2,1,0:T(8,128)(2,1)S(1)}, bf16[2,128,512]{2,1,0:T(8,128)(2,1)}, u32[]{:S(2)}, u32[]{:S(2)}) collective-permute-start(bf16[2,128,512]{2,1,0:T(8,128)(2,1)S(1)} %copy.364), channel_id=1, source_target_pairs={{0,1},{1,2},{2,3},{3,0},{4,5},{5,6},{6,7},{7,4},{8,9},{9,10},{10,1... | collective-permute-start | bytes 786440 | tf_op jit(solution)/shard_map/while/body/eval_jaxpr/ppermute | solution.py:11
  412.2 6.5 %copy-start.14 = (bf16[64,4,128]{2,1,0:T(4,128)(2,1)S(1)}, bf16[64,4,128]{2,1,0:T(4,128)(2,1)}, u32[]{:S(2)}) copy-start(bf16[64,4,128]{2,1,0:T(4,128)(2,1)} %squeeze.378) | copy-start | bytes 196612 | tf_op jit(solution)/shard_map/while
  412.2 6.5 %copy-start.17 = (bf16[64,4,128]{2,1,0:T(4,128)(2,1)S(1)}, bf16[64,4,128]{2,1,0:T(4,128)(2,1)}, u32[]{:S(2)}) copy-start(bf16[64,4,128]{2,1,0:T(4,128)(2,1)} %squeeze.379) | copy-start | bytes 196612 | tf_op jit(solution)/shard_map/while
  412.2 6.5 %copy-start.38 = (f32[2,4,8,64]{3,2,1,0:T(8,128)S(1)}, f32[2,4,8,64]{3,2,1,0:T(8,128)}, u32[]{:S(2)}) copy-start(f32[2,4,8,64]{3,2,1,0:T(8,128)} %get-tuple-element.2867) | copy-start | bytes 49156 | tf_op jit(solution)/shard_map/while
  412.2 6.5 %copy-start.39 = (f32[2,4,8,64]{3,2,1,0:T(8,128)S(1)}, f32[2,4,8,64]{3,2,1,0:T(8,128)}, u32[]{:S(2)}) copy-start(f32[2,4,8,64]{3,2,1,0:T(8,128)} %get-tuple-element.2866) | copy-start | bytes 49156 | tf_op jit(solution)/shard_map/while
  445.5 12.1 %collective-permute-start.3 = (f32[2,128,512]{2,1,0:T(8,128)}, f32[2,128,512]{2,1,0:T(8,128)}, u32[]{:S(2)}, u32[]{:S(2)}) collective-permute-start(f32[2,128,512]{2,1,0:T(8,128)} %maximum_add_fusion.10), channel_id=1, source_target_pairs={{0,1},{1,2},{2,3},{3,0},{4,5},{5,6},{6,7},{7,4},{8,9},{9,10},{10,1... | collective-permute-start | bytes 1572872 | tf_op jit(solution)/shard_map/while/body/eval_jaxpr/ppermute | solution.py:11
  445.5 12.1 %collective-permute-start.2 = (bf16[2,128,512]{2,1,0:T(8,128)(2,1)S(1)}, bf16[2,128,512]{2,1,0:T(8,128)(2,1)}, u32[]{:S(2)}, u32[]{:S(2)}) collective-permute-start(bf16[2,128,512]{2,1,0:T(8,128)(2,1)S(1)} %copy.385), channel_id=1, source_target_pairs={{0,1},{1,2},{2,3},{3,0},{4,5},{5,6},{6,7},{7,4},{8,9},{9,10},{10,1... | collective-permute-start | bytes 786440 | tf_op jit(solution)/shard_map/while/body/eval_jaxpr/ppermute | solution.py:11
  461.2 6.5 %copy-start.14 = (bf16[64,4,128]{2,1,0:T(4,128)(2,1)S(1)}, bf16[64,4,128]{2,1,0:T(4,128)(2,1)}, u32[]{:S(2)}) copy-start(bf16[64,4,128]{2,1,0:T(4,128)(2,1)} %squeeze.378) | copy-start | bytes 196612 | tf_op jit(solution)/shard_map/while
  461.2 6.5 %copy-start.17 = (bf16[64,4,128]{2,1,0:T(4,128)(2,1)S(1)}, bf16[64,4,128]{2,1,0:T(4,128)(2,1)}, u32[]{:S(2)}) copy-start(bf16[64,4,128]{2,1,0:T(4,128)(2,1)} %squeeze.379) | copy-start | bytes 196612 | tf_op jit(solution)/shard_map/while
  461.2 6.5 %copy-start.38 = (f32[2,4,8,64]{3,2,1,0:T(8,128)S(1)}, f32[2,4,8,64]{3,2,1,0:T(8,128)}, u32[]{:S(2)}) copy-start(f32[2,4,8,64]{3,2,1,0:T(8,128)} %get-tuple-element.2867) | copy-start | bytes 49156 | tf_op jit(solution)/shard_map/while
  476.4 9.9 %copy-start.28 = (f32[64,4,128]{2,0,1:T(8,128)S(1)}, f32[64,4,128]{2,0,1:T(8,128)}, u32[]{:S(2)}) copy-start(f32[64,4,128]{2,0,1:T(8,128)} %copy-done.27) | copy-start | bytes 393220 | tf_op jit(solution)/shard_map/while
  476.4 9.9 %copy-start.30 = (f32[64,4,128]{2,0,1:T(8,128)S(1)}, f32[64,4,128]{2,0,1:T(8,128)}, u32[]{:S(2)}) copy-start(f32[64,4,128]{2,0,1:T(8,128)} %copy-done.29) | copy-start | bytes 393220 | tf_op jit(solution)/shard_map/while
  490.5 12.1 %collective-permute-start.3 = (f32[2,128,512]{2,1,0:T(8,128)}, f32[2,128,512]{2,1,0:T(8,128)}, u32[]{:S(2)}, u32[]{:S(2)}) collective-permute-start(f32[2,128,512]{2,1,0:T(8,128)} %maximum_add_fusion.10), channel_id=1, source_target_pairs={{0,1},{1,2},{2,3},{3,0},{4,5},{5,6},{6,7},{7,4},{8,9},{9,10},{10,1... | collective-permute-start | bytes 1572872 | tf_op jit(solution)/shard_map/while/body/eval_jaxpr/ppermute | solution.py:11
  490.5 12.1 %collective-permute-start.2 = (bf16[2,128,512]{2,1,0:T(8,128)(2,1)S(1)}, bf16[2,128,512]{2,1,0:T(8,128)(2,1)}, u32[]{:S(2)}, u32[]{:S(2)}) collective-permute-start(bf16[2,128,512]{2,1,0:T(8,128)(2,1)S(1)} %copy.385), channel_id=1, source_target_pairs={{0,1},{1,2},{2,3},{3,0},{4,5},{5,6},{6,7},{7,4},{8,9},{9,10},{10,1... | collective-permute-start | bytes 786440 | tf_op jit(solution)/shard_map/while/body/eval_jaxpr/ppermute | solution.py:11
  506.2 6.5 %copy-start.14 = (bf16[64,4,128]{2,1,0:T(4,128)(2,1)S(1)}, bf16[64,4,128]{2,1,0:T(4,128)(2,1)}, u32[]{:S(2)}) copy-start(bf16[64,4,128]{2,1,0:T(4,128)(2,1)} %squeeze.378) | copy-start | bytes 196612 | tf_op jit(solution)/shard_map/while
  534.9 12.1 %collective-permute-start.3 = (f32[2,128,512]{2,1,0:T(8,128)}, f32[2,128,512]{2,1,0:T(8,128)}, u32[]{:S(2)}, u32[]{:S(2)}) collective-permute-start(f32[2,128,512]{2,1,0:T(8,128)} %maximum_add_fusion.10), channel_id=1, source_target_pairs={{0,1},{1,2},{2,3},{3,0},{4,5},{5,6},{6,7},{7,4},{8,9},{9,10},{10,1... | collective-permute-start | bytes 1572872 | tf_op jit(solution)/shard_map/while/body/eval_jaxpr/ppermute | solution.py:11
  534.9 12.1 %collective-permute-start.2 = (bf16[2,128,512]{2,1,0:T(8,128)(2,1)S(1)}, bf16[2,128,512]{2,1,0:T(8,128)(2,1)}, u32[]{:S(2)}, u32[]{:S(2)}) collective-permute-start(bf16[2,128,512]{2,1,0:T(8,128)(2,1)S(1)} %copy.385), channel_id=1, source_target_pairs={{0,1},{1,2},{2,3},{3,0},{4,5},{5,6},{6,7},{7,4},{8,9},{9,10},{10,1... | collective-permute-start | bytes 786440 | tf_op jit(solution)/shard_map/while/body/eval_jaxpr/ppermute | solution.py:11
  550.5 6.5 %copy-start.14 = (bf16[64,4,128]{2,1,0:T(4,128)(2,1)S(1)}, bf16[64,4,128]{2,1,0:T(4,128)(2,1)}, u32[]{:S(2)}) copy-start(bf16[64,4,128]{2,1,0:T(4,128)(2,1)} %squeeze.378) | copy-start | bytes 196612 | tf_op jit(solution)/shard_map/while
  579.2 12.1 %collective-permute-start.3 = (f32[2,128,512]{2,1,0:T(8,128)}, f32[2,128,512]{2,1,0:T(8,128)}, u32[]{:S(2)}, u32[]{:S(2)}) collective-permute-start(f32[2,128,512]{2,1,0:T(8,128)} %maximum_add_fusion.10), channel_id=1, source_target_pairs={{0,1},{1,2},{2,3},{3,0},{4,5},{5,6},{6,7},{7,4},{8,9},{9,10},{10,1... | collective-permute-start | bytes 1572872 | tf_op jit(solution)/shard_map/while/body/eval_jaxpr/ppermute | solution.py:11
  579.2 12.1 %collective-permute-start.2 = (bf16[2,128,512]{2,1,0:T(8,128)(2,1)S(1)}, bf16[2,128,512]{2,1,0:T(8,128)(2,1)}, u32[]{:S(2)}, u32[]{:S(2)}) collective-permute-start(bf16[2,128,512]{2,1,0:T(8,128)(2,1)S(1)} %copy.385), channel_id=1, source_target_pairs={{0,1},{1,2},{2,3},{3,0},{4,5},{5,6},{6,7},{7,4},{8,9},{9,10},{10,1... | collective-permute-start | bytes 786440 | tf_op jit(solution)/shard_map/while/body/eval_jaxpr/ppermute | solution.py:11
  602.5 26.4 %collective-permute-start.4 = (bf16[1,128,4096]{2,1,0:T(8,128)(2,1)S(1)}, bf16[1,128,4096]{2,1,0:T(8,128)(2,1)S(1)}, u32[]{:S(2)}, u32[]{:S(2)}) collective-permute-start(bf16[1,128,4096]{2,1,0:T(8,128)(2,1)S(1)} %fusion.148), channel_id=1, source_target_pairs={{0,28},{4,0},{8,4},{12,8},{16,12},{20,16},{24,20},{28,24},{1,29},{... | collective-permute-start | bytes 3145736 | tf_op jit(solution)/shard_map/ppermute | solution.py:11
  (115 other events, 299.9 us)
where the time goes:
time: 643 us; the launch traced here: 630 us
  local copies, waits for them, and re-layouts  193 us (30%)
  other arithmetic  157 us (24%)
  loops' own time  112 us (17%)
  waiting for transfers between devices  74.9 us (12%)
  matrix products  57.3 us (9%)
  starting transfers between devices  17.1 us (3%)
  blocking collectives  16 us (2%)
    ppermute x17, waiting for transfers between devices, shifted(): lax.ppermute(array, axis, [(i, (i + by) % length) for i in range(length)])  74.9 us
    another operation x2, loops' own time, on_device(): lax.fori_loop(0, cycle_size, cycle_step, (key_values, jnp.zeros((2, token...  41.4 us
    another operation x2, loops' own time, on_device(): lax.fori_loop(0, key_piece.shape[0] // tokens, piece_step, initial)  39.1 us
    while x296, local copies, waits for them, and re-layouts  36.4 us
    add x8, other arithmetic, cycle_step(): return (travel_block, travel_grads, query_acc + query_part_grad)  23.3 us
    add x16, other arithmetic, gradient_shard(): query_grads[query_part] = query_grads[query_part] + query_grad  21.8 us
    add x16, other arithmetic, gradient_shard(): key_grads[key_part] = key_grads[key_part] + key_grad  21.5 us
    add x8, other arithmetic, cycle_step(): travel_grads = travel_grads + key_part_grad  17.1 us
  transfers between devices with their start and end apart: 17, of which 9 were waited for; matrix products, arithmetic and copies ran while one was open for 7% of the time, Pallas kernels for 0%

commit v1 on v0

v1 whole, which is shorter than its diff:
```python
import functools
import math

import jax
import jax.numpy as jnp
from jax import lax
from jax.experimental import pallas as pl
from jax.experimental.pallas import tpu as pltpu
from jax.sharding import PartitionSpec as P

DH = 128
HIDDEN = -1e30


def exchanged(array, axis, mask):
    length = lax.axis_size(axis)
    return lax.ppermute(array, axis, [(i, i ^ mask) for i in range(length)])


def shifted(array, axis, by):
    length = lax.axis_size(axis)
    return lax.ppermute(array, axis, [(i, (i + by) % length) for i in range(length)])


def layer_kernel(piece_count, targets, repeat, meta_ref, q_ref, g_ref, o_ref, *refs):
    pieces = refs[:piece_count]
    g_out_ref = refs[piece_count]
    outs = refs[piece_count + 1 : piece_count + 1 + len(targets)]
    p_s, ds_s = refs[-2:]
    tokens = q_ref.shape[0]
    span_rows = tokens // 2
    keys_total = p_s.shape[0]
    scale = DH ** (-0.5)
    pair = 2 * DH
    pair_rows = 2 * tokens

    @pl.when(meta_ref[0] == 0)
    def _():
        g_out_ref[...] = g_ref[...]
        for out in outs:
            out[...] = jnp.zeros_like(out)

    @pl.when(meta_ref[0] != 0)
    def _():
        keys = jnp.concatenate([piece[0] for piece in pieces], axis=0)
        values = jnp.concatenate([piece[1] for piece in pieces], axis=0)
        keys_t = keys.T
        lane = lax.broadcasted_iota(jnp.int32, (span_rows, tokens), 1)
        query_pos = jnp.where(
            lane < span_rows,
            meta_ref[1] * span_rows + lane,
            meta_ref[2] * span_rows + lane - span_rows,
        )
        row = lax.broadcasted_iota(jnp.int32, (span_rows, tokens), 0)
        bias = jnp.concatenate(
            [
                jnp.where(meta_ref[3 + t] * span_rows + row <= query_pos, 0.0, HIDDEN)
                for t in range(keys_total // span_rows)
            ],
            axis=0,
        )
        bias = jnp.concatenate([bias, bias], axis=1)
        ones = jnp.ones((8, 2 * DH), jnp.bfloat16)

        def heads_of(ref, index):
            return jnp.concatenate(
                [
                    ref[:, pl.ds(index * pair, DH)],
                    ref[:, pl.ds(index * pair + DH, DH)],
                ],
                axis=0,
            )

        def visit(index):
            q2 = heads_of(q_ref, index)
            g2 = heads_of(g_ref, index)
            o2 = heads_of(o_ref, index)
            product = g2.astype(jnp.float32) * o2.astype(jnp.float32)
            high = product.astype(jnp.bfloat16)
            low = (product - high.astype(jnp.float32)).astype(jnp.bfloat16)
            nt = (((1,), (1,)), ((), ()))
            row_dot = lax.dot_general(
                ones,
                jnp.concatenate([high, low], axis=1),
                nt,
                preferred_element_type=jnp.float32,
            )[0:1]
            scores = lax.dot_general(keys, q2, nt, preferred_element_type=jnp.float32)
            scores = scores + bias
            top = jnp.max(scores, axis=0, keepdims=True)
            factor = scale * math.log2(math.e)
            powers = jnp.exp2(scores * factor - top * factor)
            inverse = 1.0 / jnp.sum(powers, axis=0, keepdims=True)
            probs = (powers * inverse).astype(jnp.bfloat16)
            grad_probs = lax.dot_general(values, g2, nt, preferred_element_type=jnp.float32)
            grad_scores = (probs.astype(jnp.float32) * (grad_probs - row_dot)).astype(jnp.bfloat16)
            columns = pl.ds(index * pair_rows, pair_rows)
            p_s[:, columns] = probs
            ds_s[:, columns] = grad_scores
            query_grad = lax.dot_general(
                keys_t, grad_scores, (((1,), (0,)), ((), ())), preferred_element_type=jnp.float32
            )
            query_grad = query_grad.T * scale
            for part in range(2):
                lanes = pl.ds(index * pair + part * DH, DH)
                g_out_ref[:, lanes] = (
                    g_ref[:, lanes].astype(jnp.float32)
                    + query_grad[part * tokens : (part + 1) * tokens]
                ).astype(g_out_ref.dtype)

        if keys_total <= 512:
            for index in range(repeat // 2):
                visit(index)
        else:

            @pl.loop(0, repeat // 2)
            def _(index):
                visit(index)

        q_all = jnp.concatenate([q_ref[:, r * DH : (r + 1) * DH] for r in range(repeat)], axis=0)
        g_all = jnp.concatenate([g_ref[:, r * DH : (r + 1) * DH] for r in range(repeat)], axis=0)
        value_grad = jnp.dot(p_s[...], g_all, preferred_element_type=jnp.float32)
        key_grad = jnp.dot(ds_s[...], q_all, preferred_element_type=jnp.float32) * scale
        for out, ranges in zip(outs, targets):
            at = 0
            for start, size in ranges:
                out[0, at : at + size] = key_grad[start : start + size].astype(out.dtype)
                out[1, at : at + size] = value_grad[start : start + size].astype(out.dtype)
                at += size


def layer(meta, queries, gradient, saved_out, slot, pieces, targets, dtypes):
    tokens, width = gradient.shape
    kv_width = pieces[0].shape[-1]
    groups = kv_width // DH
    repeat = width // kv_width
    keys_total = sum(piece.shape[-2] for piece in pieces)
    head_block = pl.BlockSpec((None, None, tokens, repeat * DH), lambda e: (0, slot, 0, e))
    grad_block = pl.BlockSpec((tokens, repeat * DH), lambda e: (0, e))
    piece_specs = []
    for piece in pieces:
        if piece.ndim == 5:
            piece_specs.append(
                pl.BlockSpec((None, None, 2, piece.shape[3], DH), lambda e: (0, slot, 0, 0, e))
            )
        else:
            piece_specs.append(pl.BlockSpec((2, piece.shape[1], DH), lambda e: (0, 0, e)))
    rows = [sum(size for _, size in ranges) for ranges in targets]
    outs = pl.pallas_call(
        functools.partial(layer_kernel, len(pieces), targets, repeat),
        grid=(groups,),
        in_specs=[
            pl.BlockSpec(memory_space=pltpu.SMEM),
            head_block,
            grad_block,
            head_block,
            *piece_specs,
        ],
        out_specs=[grad_block]
        + [pl.BlockSpec((2, count, DH), lambda e: (0, 0, e)) for count in rows],
        out_shape=[jax.ShapeDtypeStruct((tokens, width), jnp.bfloat16)]
        + [
            jax.ShapeDtypeStruct((2, count, kv_width), dtype) for count, dtype in zip(rows, dtypes)
        ],
        scratch_shapes=[
            pltpu.VMEM((keys_total, repeat * tokens), jnp.bfloat16),
            pltpu.VMEM((keys_total, repeat * tokens), jnp.bfloat16),
        ],
        compiler_params=pltpu.CompilerParams(vmem_limit_bytes=48 << 20),
        cost_estimate=pl.CostEstimate(
            flops=10 * tokens * width * keys_total,
            bytes_accessed=10 * tokens * width,
            transcendentals=tokens * (width // DH) * keys_total,
        ),
        name=f"layer_{slot}",
    )(meta, queries, gradient, saved_out, *pieces)
    return outs


def on_device(queries, keyvals, saved_out, grad_in, section_layers, span_order):
    cycle = lax.axis_size("ctx")
    own = lax.axis_index("ctx")
    section = lax.axis_index("section")
    slots = queries.shape[1]
    tokens = queries.shape[2]
    half = tokens // 2
    order_rows = span_order.reshape(cycle, 2)
    layer_count = lax.dynamic_index_in_dim(section_layers, section, 0, keepdims=False)
    own_spans = lax.dynamic_index_in_dim(order_rows, own, 0, keepdims=False)
    square = cycle == 4

    if square:
        sources = jnp.stack([own, own ^ 1, own ^ 2, own ^ 3])
        key_spans = order_rows[sources].reshape(-1)
    else:
        key_spans = span_order

    def gathered(slot):
        if not square:
            return [lax.all_gather(keyvals[0, slot], "ctx", axis=1, tiled=True)]
        block = keyvals[0, slot]
        from_x = exchanged(block, "ctx", 1)
        from_y = exchanged(block, "ctx", 2)
        low = exchanged(from_y[:, :half], "ctx", 1)
        high = exchanged(from_x[:, half:], "ctx", 2)
        return [keyvals, from_x, from_y, low, high]

    if square:
        targets = (
            ((0, tokens),),
            ((3 * tokens, half), (tokens, half)),
            ((3 * tokens + half, half), (2 * tokens + half, half)),
            ((tokens + half, half),),
            ((2 * tokens, half),),
        )
        dtypes = (jnp.float32, jnp.bfloat16, jnp.bfloat16, jnp.float32, jnp.float32)
    else:
        targets = (((0, cycle * tokens),),)
        dtypes = (jnp.float32,)

    def reduced(parts):
        if not square:
            total = lax.psum_scatter(parts[0], "ctx", scatter_dimension=1, tiled=True)
            return total.astype(jnp.bfloat16)
        mine, first_x, first_y, rest_x, rest_y = parts
        got_x = exchanged(first_x, "ctx", 1)
        got_y = exchanged(first_y, "ctx", 2)
        second_x = (rest_x + got_y[:, :half].astype(jnp.float32)).astype(jnp.bfloat16)
        second_y = (rest_y + got_x[:, :half].astype(jnp.float32)).astype(jnp.bfloat16)
        more_x = exchanged(second_x, "ctx", 1)
        more_y = exchanged(second_y, "ctx", 2)
        low = (
            mine[:, :half]
            + got_x[:, half:].astype(jnp.float32)
            + more_y.astype(jnp.float32)
        )
        high = (
            mine[:, half:]
            + got_y[:, half:].astype(jnp.float32)
            + more_x.astype(jnp.float32)
        )
        return jnp.concatenate([low, high], axis=1).astype(jnp.bfloat16)

    gradient = grad_in[0]
    results = [None] * slots
    pieces = {slot: gathered(slot) for slot in reversed(range(slots))}
    for slot in reversed(range(slots)):
        live = (slot < layer_count).astype(jnp.int32)
        meta = jnp.concatenate([live[None], own_spans, key_spans]).astype(jnp.int32)
        gradient, *parts = layer(
            meta, queries, gradient, saved_out, slot, pieces[slot], targets, dtypes
        )
        results[slot] = reduced(parts)
    grad_kv = jnp.stack(results)[None]
    grad_down = shifted(gradient[None], "section", -1)
    return (grad_kv, grad_down)


def solution(mesh):
    in_specs = (
        P("section", None, "ctx", None),
        P("section", None, None, "ctx", None),
        P("section", None, "ctx", None),
        P("section", "ctx", None),
        P(),
        P(),
    )
    out_specs = (P("section", None, None, "ctx", None), P("section", "ctx", None))
    return jax.shard_map(
        on_device, mesh=mesh, in_specs=in_specs, out_specs=out_specs, check_vma=False
    )
```

time: 643 us -> 66.2 us (0.10)
  the two profiles are of different devices: /device:TPU:13 before, /device:TPU:9 now
where the time goes in v1:
time: 66.2 us; the launch traced here: 65.5 us
  Pallas kernels  25 us (38%)
  waiting for transfers between devices  17.8 us (27%)
  starting transfers between devices  14.5 us (22%)
  local copies, waits for them, and re-layouts  4.82 us (7%)
  between operations  2.03 us (3%)
  other arithmetic  1.33 us (2%)
    pallas_call x2, Pallas kernels, layer(): pl.pallas_call(functools.partial(layer_kernel, len(pieces), targets, repe...  25 us
    ppermute x16, starting transfers between devices, exchanged(): return lax.ppermute(array, axis, [(i, i ^ mask) for i in range(length)])  14.5 us
    ppermute x16, waiting for transfers between devices, exchanged(): return lax.ppermute(array, axis, [(i, i ^ mask) for i in range(length)])  10.9 us
    ppermute x1, waiting for transfers between devices, shifted(): lax.ppermute(array, axis, [(i, (i + by) % length) for i in range(length)])  6.95 us
  transfers between devices with their start and end apart: 17, of which 7 were waited for; matrix products, arithmetic and copies ran while one was open for 6% of the time, Pallas kernels for 38%

profile of v1, /device:TPU:9, one launch (start us, length us, event | category | flops | bytes accessed | tf_op | source)
XLA Modules:
  0.0 65.5 jit_solution(13726128635241261249)
XLA Ops:
  0.6 0.0 copy-start
  0.6 1.2 %slice_bitcast_fusion = (bf16[2,128,512]{2,1,0:T(8,128)(2,1)S(1)}, bf16[2,128,512]{2,1,0:T(8,128)(2,1)S(1)}) fusion(bf16[1,2,2,128,512]{4,3,2,1,0:T(8,128)(2,1)} %refs_0_.3), kind=kLoop, calls=%fused_computation.10 | loop fusion | bytes 1048576 | tf_op jit(solution)/shard_map/squeeze | solution.py:201
  1.8 1.3 %collective-permute-start.1 = (bf16[2,128,512]{2,1,0:T(8,128)(2,1)S(1)}, bf16[2,128,512]{2,1,0:T(8,128)(2,1)S(1)}, u32[]{:S(2)}, u32[]{:S(2)}) collective-permute-start(bf16[2,128,512]{2,1,0:T(8,128)(2,1)S(1)} %get-tuple-element.29), channel_id=1, source_target_pairs={{0,2},{1,3},{2,0},{3,1},{4,6},{5,7},{6,4},{7,5},{8,10},{9,11},{10,... | collective-permute-start | bytes 786440 | tf_op jit(solution)/shard_map/ppermute | solution.py:17
  3.1 1.2 %collective-permute-start = (bf16[2,128,512]{2,1,0:T(8,128)(2,1)S(1)}, bf16[2,128,512]{2,1,0:T(8,128)(2,1)S(1)}, u32[]{:S(2)}, u32[]{:S(2)}) collective-permute-start(bf16[2,128,512]{2,1,0:T(8,128)(2,1)S(1)} %get-tuple-element.29), channel_id=1, source_target_pairs={{0,1},{1,0},{2,3},{3,2},{4,5},{5,4},{6,7},{7,6},{8,9},{9,8},{10,11... | collective-permute-start | bytes 786440 | tf_op jit(solution)/shard_map/ppermute | solution.py:17
  4.3 0.2 collective-permute-start.5
  4.6 0.3 collective-permute-start.4
  4.8 0.1 fusion.4
  4.9 0.7 %reshape.241 = s32[4,2]{1,0:T(4,128)S(1)} reshape(s32[8]{0:T(128)} %param.11) | data formatting | bytes 64 | tf_op jit(solution)/shard_map/reshape | solution.py:187
  5.7 3.4 %collective-permute-done.1.refs_2_ = bf16[2,128,512]{2,1,0:T(8,128)(2,1)S(1)} collective-permute-done((bf16[2,128,512]{2,1,0:T(8,128)(2,1)S(1)}, bf16[2,128,512]{2,1,0:T(8,128)(2,1)S(1)}, u32[]{:S(2)}, u32[]{:S(2)}) %collective-permute-start.1) | collective-permute-done | bytes 262176 | tf_op jit(solution)/shard_map/ppermute | solution.py:17
  9.1 1.3 %collective-permute-start.2 = (bf16[2,64,512]{2,1,0:T(8,128)(2,1)S(1)}, bf16[2,64,512]{2,1,0:T(8,128)(2,1)S(1)}, u32[]{:S(2)}, u32[]{:S(2)}) collective-permute-start(bf16[2,64,512]{2,1,0:T(8,128)(2,1)S(1)} %slice.74), channel_id=1, source_target_pairs={{0,1},{1,0},{2,3},{3,2},{4,5},{5,4},{6,7},{7,6},{8,9},{9,8},{10,11... | collective-permute-start | bytes 393224 | tf_op jit(solution)/shard_map/ppermute | solution.py:17
  10.4 0.0 collective-permute-done.refs_1_
  10.4 1.3 %collective-permute-start.3 = (bf16[2,64,512]{2,1,0:T(8,128)(2,1)S(1)}, bf16[2,64,512]{2,1,0:T(8,128)(2,1)S(1)}, u32[]{:S(2)}, u32[]{:S(2)}) collective-permute-start(bf16[2,64,512]{2,1,0:T(8,128)(2,1)S(1)} %slice.75), channel_id=1, source_target_pairs={{0,2},{1,3},{2,0},{3,1},{4,6},{5,7},{6,4},{7,5},{8,10},{9,11},{10,... | collective-permute-start | bytes 393224 | tf_op jit(solution)/shard_map/ppermute | solution.py:17
  11.7 1.2 %dynamic_slice.8 = s32[1]{0:T(128)} dynamic-slice(s32[8]{0:T(128)} %param.10, s32[]{:T(128)S(6)} %select_n.18), dynamic_slice_sizes={1} | dynamic-slice | bytes 12 | tf_op jit(solution)/shard_map/jit(dynamic_index_in_dim)/dynamic_slice | solution.py:188
  14.2 0.6 gather_fusion
  14.8 0.1 reshape.242
  14.9 0.1 add_add_fusion
  15.0 0.0 collective-permute-done.5.refs_2_
  15.0 1.0 %collective-permute-start.6 = (bf16[2,64,512]{2,1,0:T(8,128)(2,1)S(1)}, bf16[2,64,512]{2,1,0:T(8,128)(2,1)S(1)}, u32[]{:S(2)}, u32[]{:S(2)}) collective-permute-start(bf16[2,64,512]{2,1,0:T(8,128)(2,1)S(1)} %slice.76), channel_id=1, source_target_pairs={{0,1},{1,0},{2,3},{3,2},{4,5},{5,4},{6,7},{7,6},{8,9},{9,8},{10,11... | collective-permute-start | bytes 393224 | tf_op jit(solution)/shard_map/ppermute | solution.py:17
  16.0 0.0 collective-permute-done.4.refs_1_
  16.0 1.3 %collective-permute-start.7 = (bf16[2,64,512]{2,1,0:T(8,128)(2,1)S(1)}, bf16[2,64,512]{2,1,0:T(8,128)(2,1)S(1)}, u32[]{:S(2)}, u32[]{:S(2)}) collective-permute-start(bf16[2,64,512]{2,1,0:T(8,128)(2,1)S(1)} %slice.77), channel_id=1, source_target_pairs={{0,2},{1,3},{2,0},{3,1},{4,6},{5,7},{6,4},{7,5},{8,10},{9,11},{10,... | collective-permute-start | bytes 393224 | tf_op jit(solution)/shard_map/ppermute | solution.py:17
  17.3 1.1 %collective-permute-done.2.refs_3_ = bf16[2,64,512]{2,1,0:T(8,128)(2,1)S(1)} collective-permute-done((bf16[2,64,512]{2,1,0:T(8,128)(2,1)S(1)}, bf16[2,64,512]{2,1,0:T(8,128)(2,1)S(1)}, u32[]{:S(2)}, u32[]{:S(2)}) %collective-permute-start.2) | collective-permute-done | bytes 131104 | tf_op jit(solution)/shard_map/ppermute | solution.py:17
  18.4 0.0 collective-permute-done.3.refs_4_
  18.4 12.5 %layer_1.1 = (bf16[128,4096]{1,0:T(8,128)(2,1)S(1)}, f32[2,128,512]{2,1,0:T(8,128)S(1)}, bf16[2,128,512]{2,1,0:T(8,128)(2,1)S(1)}, bf16[2,128,512]{2,1,0:T(8,128...) custom-call(s32[11]{0:T(128)S(1)} %get-tuple-element.33.meta_ref, bf16[1,2,128,4096]{3,2,1,0:T(8,128)(2,1)} %q_ref.3, ...), custom_call_target="tpu_custom_call" | custom-call | flops 2684354560 | bytes 5242880 | tf_op jit(solution)/shard_map/layer_1/pallas_call | solution.py:149
  30.9 1.3 %collective-permute-start.12 = (bf16[2,128,512]{2,1,0:T(8,128)(2,1)S(1)}, bf16[2,128,512]{2,1,0:T(8,128)(2,1)S(1)}, u32[]{:S(2)}, u32[]{:S(2)}) collective-permute-start(bf16[2,128,512]{2,1,0:T(8,128)(2,1)S(1)} %get-tuple-element.21), channel_id=1, source_target_pairs={{0,1},{1,0},{2,3},{3,2},{4,5},{5,4},{6,7},{7,6},{8,9},{9,8},{10,11... | collective-permute-start | bytes 786440 | tf_op jit(solution)/shard_map/ppermute | solution.py:17
  32.2 0.3 collective-permute-start.14
  32.5 0.0 collective-permute-done.6.refs_3_
  32.5 0.0 collective-permute-done.7.refs_4_
  32.5 12.5 %layer_0.1 = (bf16[128,4096]{1,0:T(8,128)(2,1)S(1)}, f32[2,128,512]{2,1,0:T(8,128)S(1)}, bf16[2,128,512]{2,1,0:T(8,128)(2,1)S(1)}, bf16[2,128,512]{2,1,0:T(8,128...) custom-call(s32[11]{0:T(128)S(1)} %get-tuple-element.32.meta_ref, bf16[1,2,128,4096]{3,2,1,0:T(8,128)(2,1)} %q_ref.3, ...), custom_call_target="tpu_custom_call" | custom-call | flops 2684354560 | bytes 5242880 | tf_op jit(solution)/shard_map/layer_0/pallas_call | solution.py:149
  45.0 0.3 collective-permute-start.8
  45.3 1.2 %collective-permute-start.10 = (bf16[2,128,512]{2,1,0:T(8,128)(2,1)S(1)}, bf16[2,128,512]{2,1,0:T(8,128)(2,1)S(1)}, u32[]{:S(2)}, u32[]{:S(2)}) collective-permute-start(bf16[2,128,512]{2,1,0:T(8,128)(2,1)S(1)} %get-tuple-element.18), channel_id=1, source_target_pairs={{0,2},{1,3},{2,0},{3,1},{4,6},{5,7},{6,4},{7,5},{8,10},{9,11},{10,... | collective-permute-start | bytes 786440 | tf_op jit(solution)/shard_map/ppermute | solution.py:17
  46.5 0.0 collective-permute-start.16
  46.5 0.0 collective-permute-done.12
  46.6 0.4 collective-permute-start.13
  46.9 0.0 collective-permute-done.14
  47.0 1.3 %collective-permute-start.15 = (bf16[2,64,512]{2,1,0:T(8,128)(2,1)S(1)}, bf16[2,64,512]{2,1,0:T(8,128)(2,1)S(1)}, u32[]{:S(2)}, u32[]{:S(2)}) collective-permute-start(bf16[2,64,512]{2,1,0:T(8,128)(2,1)S(1)} %add_convert_fusion.1), channel_id=1, source_target_pairs={{0,1},{1,0},{2,3},{3,2},{4,5},{5,4},{6,7},{7,6},{8,9},{9,8},{10,11... | collective-permute-start | bytes 393224 | tf_op jit(solution)/shard_map/ppermute | solution.py:17
  48.2 2.4 %collective-permute-done.8 = bf16[2,128,512]{2,1,0:T(8,128)(2,1)S(1)} collective-permute-done((bf16[2,128,512]{2,1,0:T(8,128)(2,1)S(1)}, bf16[2,128,512]{2,1,0:T(8,128)(2,1)S(1)}, u32[]{:S(2)}, u32[]{:S(2)}) %collective-permute-start.8) | collective-permute-done | bytes 262176 | tf_op jit(solution)/shard_map/ppermute | solution.py:17
  50.6 1.2 %collective-permute-start.9 = (bf16[2,64,512]{2,1,0:T(8,128)(2,1)S(1)}, bf16[2,64,512]{2,1,0:T(8,128)(2,1)S(1)}, u32[]{:S(2)}, u32[]{:S(2)}) collective-permute-start(bf16[2,64,512]{2,1,0:T(8,128)(2,1)S(1)} %add_convert_fusion.7), channel_id=1, source_target_pairs={{0,2},{1,3},{2,0},{3,1},{4,6},{5,7},{6,4},{7,5},{8,10},{9,11},{10,... | collective-permute-start | bytes 393224 | tf_op jit(solution)/shard_map/ppermute | solution.py:17
  51.9 0.0 collective-permute-done.10
  51.9 0.7 %collective-permute-start.11 = (bf16[2,64,512]{2,1,0:T(8,128)(2,1)S(1)}, bf16[2,64,512]{2,1,0:T(8,128)(2,1)S(1)}, u32[]{:S(2)}, u32[]{:S(2)}) collective-permute-start(bf16[2,64,512]{2,1,0:T(8,128)(2,1)S(1)} %add_convert_fusion.5), channel_id=1, source_target_pairs={{0,1},{1,0},{2,3},{3,2},{4,5},{5,4},{6,7},{7,6},{8,9},{9,8},{10,11... | collective-permute-start | bytes 393224 | tf_op jit(solution)/shard_map/ppermute | solution.py:17
  52.6 1.5 %collective-permute-done.13 = bf16[2,64,512]{2,1,0:T(8,128)(2,1)S(1)} collective-permute-done((bf16[2,64,512]{2,1,0:T(8,128)(2,1)S(1)}, bf16[2,64,512]{2,1,0:T(8,128)(2,1)S(1)}, u32[]{:S(2)}, u32[]{:S(2)}) %collective-permute-start.13) | collective-permute-done | bytes 131104 | tf_op jit(solution)/shard_map/ppermute | solution.py:17
  54.1 0.0 collective-permute-done.15
  54.1 0.1 fusion.2
  54.2 2.2 %collective-permute-done.9 = bf16[2,64,512]{2,1,0:T(8,128)(2,1)S(1)} collective-permute-done((bf16[2,64,512]{2,1,0:T(8,128)(2,1)S(1)}, bf16[2,64,512]{2,1,0:T(8,128)(2,1)S(1)}, u32[]{:S(2)}, u32[]{:S(2)}) %collective-permute-start.9) | collective-permute-done | bytes 131104 | tf_op jit(solution)/shard_map/ppermute | solution.py:17
  56.5 0.2 collective-permute-done.11
  56.7 0.1 fusion
  56.8 0.8 %maximum_bitcast_fusion = bf16[1,2,2,128,512]{4,3,2,1,0:T(8,128)(2,1)} fusion(bf16[1,2,64,512]{3,2,1,0:T(8,128)(2,1)S(1)} %get-tuple-element.31, bf16[1,2,64,512]{3,2,1,0:T(8,128)(2,1)S(1)} %get-tuple-element.30, bf16[1,2,64,512]{3,2,1,0:T(8,128)(2,1)S(1)} %get-tuple-element.27, bf16[1,2,64,512]{3,2,1,0:T(8,128)(2,1)S(1)} %get-tuple-element.26), kind=kLoop, calls=%fused_computation.1 | loop fusion | flops 2097152 | bytes 1048576 | tf_op jit(solution)/shard_map/broadcast_in_dim | solution.py:254
  57.6 6.9 %collective-permute-done.16 = bf16[1,128,4096]{2,1,0:T(8,128)(2,1)S(1)} collective-permute-done((bf16[1,128,4096]{2,1,0:T(8,128)(2,1)S(1)}, bf16[1,128,4096]{2,1,0:T(8,128)(2,1)S(1)}, u32[]{:S(2)}, u32[]{:S(2)}) %collective-permute-start.16) | collective-permute-done | bytes 1048608 | tf_op jit(solution)/shard_map/ppermute | solution.py:22
  64.6 1.0 %copy.9 = bf16[1,128,4096]{2,1,0:T(8,128)(2,1)} copy(bf16[1,128,4096]{2,1,0:T(8,128)(2,1)S(1)} %collective-permute-done.16) | data formatting | bytes 2097152
  (13 shorter events, 0.2 us)
Async XLA Ops:
  0.6 17.8 %copy-start = (bf16[1,2,2,128,512]{4,3,2,1,0:T(8,128)(2,1)S(1)}, bf16[1,2,2,128,512]{4,3,2,1,0:T(8,128)(2,1)}, u32[]{:S(2)}) copy-start(bf16[1,2,2,128,512]{4,3,2,1,0:T(8,128)(2,1)} %refs_0_.3) | copy-start | bytes 1572868
  0.6 17.8 %copy-start.1 = (bf16[1,128,4096]{2,1,0:T(8,128)(2,1)S(1)}, bf16[1,128,4096]{2,1,0:T(8,128)(2,1)}, u32[]{:S(2)}) copy-start(bf16[1,128,4096]{2,1,0:T(8,128)(2,1)} %param.9) | copy-start | bytes 3145732
  1.8 7.2 %collective-permute-start.1 = (bf16[2,128,512]{2,1,0:T(8,128)(2,1)S(1)}, bf16[2,128,512]{2,1,0:T(8,128)(2,1)S(1)}, u32[]{:S(2)}, u32[]{:S(2)}) collective-permute-start(bf16[2,128,512]{2,1,0:T(8,128)(2,1)S(1)} %get-tuple-element.29), channel_id=1, source_target_pairs={{0,2},{1,3},{2,0},{3,1},{4,6},{5,7},{6,4},{7,5},{8,10},{9,11},{10,... | collective-permute-start | bytes 786440 | tf_op jit(solution)/shard_map/ppermute | solution.py:17
  3.1 7.2 %collective-permute-start = (bf16[2,128,512]{2,1,0:T(8,128)(2,1)S(1)}, bf16[2,128,512]{2,1,0:T(8,128)(2,1)S(1)}, u32[]{:S(2)}, u32[]{:S(2)}) collective-permute-start(bf16[2,128,512]{2,1,0:T(8,128)(2,1)S(1)} %get-tuple-element.29), channel_id=1, source_target_pairs={{0,1},{1,0},{2,3},{3,2},{4,5},{5,4},{6,7},{7,6},{8,9},{9,8},{10,11... | collective-permute-start | bytes 786440 | tf_op jit(solution)/shard_map/ppermute | solution.py:17
  4.3 10.6 %collective-permute-start.5 = (bf16[2,128,512]{2,1,0:T(8,128)(2,1)S(1)}, bf16[2,128,512]{2,1,0:T(8,128)(2,1)S(1)}, u32[]{:S(2)}, u32[]{:S(2)}) collective-permute-start(bf16[2,128,512]{2,1,0:T(8,128)(2,1)S(1)} %get-tuple-element.28), channel_id=1, source_target_pairs={{0,2},{1,3},{2,0},{3,1},{4,6},{5,7},{6,4},{7,5},{8,10},{9,11},{10,... | collective-permute-start | bytes 786440 | tf_op jit(solution)/shard_map/ppermute | solution.py:17
  4.6 11.4 %collective-permute-start.4 = (bf16[2,128,512]{2,1,0:T(8,128)(2,1)S(1)}, bf16[2,128,512]{2,1,0:T(8,128)(2,1)S(1)}, u32[]{:S(2)}, u32[]{:S(2)}) collective-permute-start(bf16[2,128,512]{2,1,0:T(8,128)(2,1)S(1)} %get-tuple-element.28), channel_id=1, source_target_pairs={{0,1},{1,0},{2,3},{3,2},{4,5},{5,4},{6,7},{7,6},{8,9},{9,8},{10,11... | collective-permute-start | bytes 786440 | tf_op jit(solution)/shard_map/ppermute | solution.py:17
  9.1 9.3 %collective-permute-start.2 = (bf16[2,64,512]{2,1,0:T(8,128)(2,1)S(1)}, bf16[2,64,512]{2,1,0:T(8,128)(2,1)S(1)}, u32[]{:S(2)}, u32[]{:S(2)}) collective-permute-start(bf16[2,64,512]{2,1,0:T(8,128)(2,1)S(1)} %slice.74), channel_id=1, source_target_pairs={{0,1},{1,0},{2,3},{3,2},{4,5},{5,4},{6,7},{7,6},{8,9},{9,8},{10,11... | collective-permute-start | bytes 393224 | tf_op jit(solution)/shard_map/ppermute | solution.py:17
  10.4 8.0 %collective-permute-start.3 = (bf16[2,64,512]{2,1,0:T(8,128)(2,1)S(1)}, bf16[2,64,512]{2,1,0:T(8,128)(2,1)S(1)}, u32[]{:S(2)}, u32[]{:S(2)}) collective-permute-start(bf16[2,64,512]{2,1,0:T(8,128)(2,1)S(1)} %slice.75), channel_id=1, source_target_pairs={{0,2},{1,3},{2,0},{3,1},{4,6},{5,7},{6,4},{7,5},{8,10},{9,11},{10,... | collective-permute-start | bytes 393224 | tf_op jit(solution)/shard_map/ppermute | solution.py:17
  15.0 17.6 %collective-permute-start.6 = (bf16[2,64,512]{2,1,0:T(8,128)(2,1)S(1)}, bf16[2,64,512]{2,1,0:T(8,128)(2,1)S(1)}, u32[]{:S(2)}, u32[]{:S(2)}) collective-permute-start(bf16[2,64,512]{2,1,0:T(8,128)(2,1)S(1)} %slice.76), channel_id=1, source_target_pairs={{0,1},{1,0},{2,3},{3,2},{4,5},{5,4},{6,7},{7,6},{8,9},{9,8},{10,11... | collective-permute-start | bytes 393224 | tf_op jit(solution)/shard_map/ppermute | solution.py:17
  16.0 16.5 %collective-permute-start.7 = (bf16[2,64,512]{2,1,0:T(8,128)(2,1)S(1)}, bf16[2,64,512]{2,1,0:T(8,128)(2,1)S(1)}, u32[]{:S(2)}, u32[]{:S(2)}) collective-permute-start(bf16[2,64,512]{2,1,0:T(8,128)(2,1)S(1)} %slice.77), channel_id=1, source_target_pairs={{0,2},{1,3},{2,0},{3,1},{4,6},{5,7},{6,4},{7,5},{8,10},{9,11},{10,... | collective-permute-start | bytes 393224 | tf_op jit(solution)/shard_map/ppermute | solution.py:17
  30.9 15.6 %collective-permute-start.12 = (bf16[2,128,512]{2,1,0:T(8,128)(2,1)S(1)}, bf16[2,128,512]{2,1,0:T(8,128)(2,1)S(1)}, u32[]{:S(2)}, u32[]{:S(2)}) collective-permute-start(bf16[2,128,512]{2,1,0:T(8,128)(2,1)S(1)} %get-tuple-element.21), channel_id=1, source_target_pairs={{0,1},{1,0},{2,3},{3,2},{4,5},{5,4},{6,7},{7,6},{8,9},{9,8},{10,11... | collective-permute-start | bytes 786440 | tf_op jit(solution)/shard_map/ppermute | solution.py:17
  32.2 14.7 %collective-permute-start.14 = (bf16[2,128,512]{2,1,0:T(8,128)(2,1)S(1)}, bf16[2,128,512]{2,1,0:T(8,128)(2,1)S(1)}, u32[]{:S(2)}, u32[]{:S(2)}) collective-permute-start(bf16[2,128,512]{2,1,0:T(8,128)(2,1)S(1)} %get-tuple-element.23), channel_id=1, source_target_pairs={{0,2},{1,3},{2,0},{3,1},{4,6},{5,7},{6,4},{7,5},{8,10},{9,11},{10,... | collective-permute-start | bytes 786440 | tf_op jit(solution)/shard_map/ppermute | solution.py:17
  45.0 5.6 %collective-permute-start.8 = (bf16[2,128,512]{2,1,0:T(8,128)(2,1)S(1)}, bf16[2,128,512]{2,1,0:T(8,128)(2,1)S(1)}, u32[]{:S(2)}, u32[]{:S(2)}) collective-permute-start(bf16[2,128,512]{2,1,0:T(8,128)(2,1)S(1)} %get-tuple-element.16), channel_id=1, source_target_pairs={{0,1},{1,0},{2,3},{3,2},{4,5},{5,4},{6,7},{7,6},{8,9},{9,8},{10,11... | collective-permute-start | bytes 786440 | tf_op jit(solution)/shard_map/ppermute | solution.py:17
  45.3 6.5 %collective-permute-start.10 = (bf16[2,128,512]{2,1,0:T(8,128)(2,1)S(1)}, bf16[2,128,512]{2,1,0:T(8,128)(2,1)S(1)}, u32[]{:S(2)}, u32[]{:S(2)}) collective-permute-start(bf16[2,128,512]{2,1,0:T(8,128)(2,1)S(1)} %get-tuple-element.18), channel_id=1, source_target_pairs={{0,2},{1,3},{2,0},{3,1},{4,6},{5,7},{6,4},{7,5},{8,10},{9,11},{10,... | collective-permute-start | bytes 786440 | tf_op jit(solution)/shard_map/ppermute | solution.py:17
  46.5 18.1 %collective-permute-start.16 = (bf16[1,128,4096]{2,1,0:T(8,128)(2,1)S(1)}, bf16[1,128,4096]{2,1,0:T(8,128)(2,1)S(1)}, u32[]{:S(2)}, u32[]{:S(2)}) collective-permute-start(bf16[1,128,4096]{2,1,0:T(8,128)(2,1)S(1)} %bitcast.25), channel_id=1, source_target_pairs={{0,28},{4,0},{8,4},{12,8},{16,12},{20,16},{24,20},{28,24},{1,29},{... | collective-permute-start | bytes 3145736 | tf_op jit(solution)/shard_map/ppermute | solution.py:22
  46.6 7.6 %collective-permute-start.13 = (bf16[2,64,512]{2,1,0:T(8,128)(2,1)S(1)}, bf16[2,64,512]{2,1,0:T(8,128)(2,1)S(1)}, u32[]{:S(2)}, u32[]{:S(2)}) collective-permute-start(bf16[2,64,512]{2,1,0:T(8,128)(2,1)S(1)} %add_convert_fusion.3), channel_id=1, source_target_pairs={{0,2},{1,3},{2,0},{3,1},{4,6},{5,7},{6,4},{7,5},{8,10},{9,11},{10,... | collective-permute-start | bytes 393224 | tf_op jit(solution)/shard_map/ppermute | solution.py:17
  47.0 7.2 %collective-permute-start.15 = (bf16[2,64,512]{2,1,0:T(8,128)(2,1)S(1)}, bf16[2,64,512]{2,1,0:T(8,128)(2,1)S(1)}, u32[]{:S(2)}, u32[]{:S(2)}) collective-permute-start(bf16[2,64,512]{2,1,0:T(8,128)(2,1)S(1)} %add_convert_fusion.1), channel_id=1, source_target_pairs={{0,1},{1,0},{2,3},{3,2},{4,5},{5,4},{6,7},{7,6},{8,9},{9,8},{10,11... | collective-permute-start | bytes 393224 | tf_op jit(solution)/shard_map/ppermute | solution.py:17
  50.6 5.8 %collective-permute-start.9 = (bf16[2,64,512]{2,1,0:T(8,128)(2,1)S(1)}, bf16[2,64,512]{2,1,0:T(8,128)(2,1)S(1)}, u32[]{:S(2)}, u32[]{:S(2)}) collective-permute-start(bf16[2,64,512]{2,1,0:T(8,128)(2,1)S(1)} %add_convert_fusion.7), channel_id=1, source_target_pairs={{0,2},{1,3},{2,0},{3,1},{4,6},{5,7},{6,4},{7,5},{8,10},{9,11},{10,... | collective-permute-start | bytes 393224 | tf_op jit(solution)/shard_map/ppermute | solution.py:17
  51.9 4.8 %collective-permute-start.11 = (bf16[2,64,512]{2,1,0:T(8,128)(2,1)S(1)}, bf16[2,64,512]{2,1,0:T(8,128)(2,1)S(1)}, u32[]{:S(2)}, u32[]{:S(2)}) collective-permute-start(bf16[2,64,512]{2,1,0:T(8,128)(2,1)S(1)} %add_convert_fusion.5), channel_id=1, source_target_pairs={{0,1},{1,0},{2,3},{3,2},{4,5},{5,4},{6,7},{7,6},{8,9},{9,8},{10,11... | collective-permute-start | bytes 393224 | tf_op jit(solution)/shard_map/ppermute | solution.py:17

commit v2 on v1

v2 whole, which is shorter than its diff:
```python
import functools
import math

import jax
import jax.numpy as jnp
from jax import lax
from jax.experimental import pallas as pl
from jax.experimental.pallas import tpu as pltpu
from jax.sharding import PartitionSpec as P

DH = 128
HIDDEN = -1e30
NT = (((1,), (1,)), ((), ()))


def exchanged(array, axis, mask):
    length = lax.axis_size(axis)
    return lax.ppermute(array, axis, [(i, i ^ mask) for i in range(length)])


def shifted(array, axis, by):
    length = lax.axis_size(axis)
    return lax.ppermute(array, axis, [(i, (i + by) % length) for i in range(length)])


def write_live(live, g_ref, g_out_ref, outs, compute):
    @pl.when(jnp.logical_not(live))
    def _():
        g_out_ref[...] = g_ref[...]
        for out in outs:
            out[...] = jnp.zeros_like(out)

    pl.when(live)(compute)


def row_dots(grads, outputs):
    product = grads.astype(jnp.float32) * outputs.astype(jnp.float32)
    return jnp.sum(product.T, axis=0, keepdims=True)


def softmax(scores):
    factor = DH ** (-0.5) * math.log2(math.e)
    top = jnp.max(scores, axis=0, keepdims=True)
    powers = jnp.exp2(scores * factor - top * factor)
    inverse = 1.0 / jnp.sum(powers, axis=0, keepdims=True)
    return (powers * inverse).astype(jnp.bfloat16)


def square_kernel(parts_of, targets, repeat, heads, slots, spans_ref, layers_ref, q_ref, g_ref, o_ref, *refs):
    pieces = refs[: len(parts_of)]
    g_out_ref = refs[len(parts_of)]
    outs = refs[len(parts_of) + 1 : len(parts_of) + 1 + len(targets)]
    g_s, k_s, v_s, dk_s, dv_s, p_hi, p_lo, ds_hi, ds_lo = refs[-9:]
    step = pl.program_id(0)
    live = layers_ref[lax.axis_index("section")] > slots - 1 - step
    span_rows = q_ref.shape[0] // 2
    spans = k_s.shape[1] // span_rows
    scale = DH ** (-0.5)
    own = lax.axis_index("ctx")

    @pl.when(step == 0)
    def _():
        g_s[...] = g_ref[...]

    @pl.when(step != 0)
    def _():
        g_s[...] = g_out_ref[...]

    def span_at(part):
        return spans_ref[2 * (own ^ part[0]) + part[1]]

    def rows_of(index):
        return pl.ds(pl.multiple_of(index * span_rows, span_rows), span_rows)

    def compute():
        for piece, parts in zip(pieces, parts_of):
            for at, part in enumerate(parts):
                rows = rows_of(span_at(part))
                for e in range(heads):
                    here = (slice(at * span_rows, (at + 1) * span_rows), slice(e * DH, (e + 1) * DH))
                    k_s[e, rows] = piece[(0, *here)]
                    v_s[e, rows] = piece[(1, *here)]
        first, second = spans_ref[2 * own], spans_ref[2 * own + 1]
        low_span = jnp.minimum(first, second)
        high_part = (second > first).astype(jnp.int32)

        def with_low(low):
            high = spans - 1 - low
            seen = (high + 1) * span_rows
            split = (low + 1) * span_rows
            shape = (span_rows, repeat * span_rows)
            offset = lax.rem(lax.broadcasted_iota(jnp.int32, shape, 1), span_rows)
            bias = jnp.where(lax.broadcasted_iota(jnp.int32, shape, 0) <= offset, 0.0, HIDDEN)

            def heads_of(ref, index, e):
                rows = rows_of(index)
                return jnp.concatenate(
                    [ref[rows, (e * repeat + r) * DH : (e * repeat + r + 1) * DH] for r in range(repeat)],
                    axis=0,
                )

            def chain(e, index, span, p_s, ds_s):
                rows = rows_of(index)
                size = (span + 1) * span_rows
                keys = k_s[e, :size]
                grads = heads_of(g_s, index, e)
                scores = lax.dot_general(
                    keys, heads_of(q_ref, index, e), NT, preferred_element_type=jnp.float32
                )
                last = scores[size - span_rows :] + bias
                if span:
                    last = jnp.concatenate([scores[: size - span_rows], last], axis=0)
                grad_probs = lax.dot_general(
                    v_s[e, :size], grads, NT, preferred_element_type=jnp.float32
                )
                dots = row_dots(grads, heads_of(o_ref, index, e))
                yield
                probs = softmax(last)
                grad_scores = (probs.astype(jnp.float32) * (grad_probs - dots)).astype(jnp.bfloat16)
                p_s[e, :size] = probs
                ds_s[e, :size] = grad_scores
                yield
                query_grad = jnp.dot(keys.T, grad_scores, preferred_element_type=jnp.float32)
                query_grad = query_grad.T * scale
                for r in range(repeat):
                    lanes = slice((e * repeat + r) * DH, (e * repeat + r + 1) * DH)
                    g_out_ref[rows, lanes] = (
                        g_s[rows, lanes].astype(jnp.float32)
                        + query_grad[r * span_rows : (r + 1) * span_rows]
                    ).astype(g_out_ref.dtype)
                yield

            def totals(e):
                for weights_hi, weights_lo, ref, total, factor in (
                    (p_hi, p_lo, g_s, dv_s, 1.0),
                    (ds_hi, ds_lo, q_ref, dk_s, scale),
                ):
                    right_hi = heads_of(ref, high_part, e)
                    right_lo = heads_of(ref, 1 - high_part, e)
                    near = jnp.dot(
                        jnp.concatenate([weights_hi[e, :split], weights_lo[e, :split]], axis=1),
                        jnp.concatenate([right_hi, right_lo], axis=0),
                        preferred_element_type=jnp.float32,
                    )
                    far = jnp.dot(
                        weights_hi[e, split:seen], right_hi, preferred_element_type=jnp.float32
                    )
                    total[e, :split] = near * factor
                    total[e, split:seen] = far * factor
                    if seen < total.shape[1]:
                        total[e, seen:] = jnp.zeros((total.shape[1] - seen, DH), jnp.float32)

            pending = None
            for e in range(heads):
                for one in (
                    chain(e, 1 - high_part, low, p_lo, ds_lo),
                    chain(e, high_part, high, p_hi, ds_hi),
                ):
                    next(one)
                    if pending is not None:
                        next(pending)
                        next(pending)
                    pending = one
                if e:
                    totals(e - 1)
            next(pending)
            next(pending)
            totals(heads - 1)

        for low in range(spans // 2):
            pl.when(low_span == low)(functools.partial(with_low, low))
        for out, parts in zip(outs, targets):
            for at, part in enumerate(parts):
                rows = rows_of(span_at(part))
                for e in range(heads):
                    here = (slice(at * span_rows, (at + 1) * span_rows), slice(e * DH, (e + 1) * DH))
                    out[(0, *here)] = dk_s[e, rows].astype(out.dtype)
                    out[(1, *here)] = dv_s[e, rows].astype(out.dtype)

    write_live(live, g_s, g_out_ref, outs, compute)


def general_kernel(
    slot, repeat, spans_ref, layers_ref, q_ref, g_ref, o_ref, piece, g_out_ref, out, p_s, ds_s
):
    tokens = q_ref.shape[0]
    span_rows = tokens // 2
    keys_total = p_s.shape[0]
    pair = 2 * DH
    own = lax.axis_index("ctx")

    def compute():
        keys = piece[0]
        values = piece[1]
        keys_t = keys.T
        lane = lax.broadcasted_iota(jnp.int32, (span_rows, tokens), 1)
        query_pos = jnp.where(
            lane < span_rows,
            spans_ref[2 * own] * span_rows + lane,
            (spans_ref[2 * own + 1] - 1) * span_rows + lane,
        )
        row = lax.broadcasted_iota(jnp.int32, (span_rows, tokens), 0)
        bias = jnp.concatenate(
            [
                jnp.where(spans_ref[t] * span_rows + row <= query_pos, 0.0, HIDDEN)
                for t in range(keys_total // span_rows)
            ],
            axis=0,
        )
        bias = jnp.concatenate([bias, bias], axis=1)

        @pl.loop(0, repeat // 2)
        def _(index):
            def heads_of(ref):
                return jnp.concatenate(
                    [ref[:, pl.ds(index * pair + part * DH, DH)] for part in range(2)], axis=0
                )

            grads = heads_of(g_ref)
            dots = row_dots(grads, heads_of(o_ref))
            scores = lax.dot_general(keys, heads_of(q_ref), NT, preferred_element_type=jnp.float32)
            probs = softmax(scores + bias)
            grad_probs = lax.dot_general(values, grads, NT, preferred_element_type=jnp.float32)
            grad_scores = (probs.astype(jnp.float32) * (grad_probs - dots)).astype(jnp.bfloat16)
            query_grad = jnp.dot(keys_t, grad_scores, preferred_element_type=jnp.float32)
            query_grad = query_grad.T * DH ** (-0.5)
            columns = pl.ds(index * 2 * tokens, 2 * tokens)
            p_s[:, columns] = probs
            ds_s[:, columns] = grad_scores
            for part in range(2):
                lanes = pl.ds(index * pair + part * DH, DH)
                g_out_ref[:, lanes] = (
                    g_ref[:, lanes].astype(jnp.float32)
                    + query_grad[part * tokens : (part + 1) * tokens]
                ).astype(g_out_ref.dtype)

        q_all = jnp.concatenate([q_ref[:, r * DH : (r + 1) * DH] for r in range(repeat)], axis=0)
        g_all = jnp.concatenate([g_ref[:, r * DH : (r + 1) * DH] for r in range(repeat)], axis=0)
        out[0] = jnp.dot(ds_s[...], q_all, preferred_element_type=jnp.float32) * DH ** (-0.5)
        out[1] = jnp.dot(p_s[...], g_all, preferred_element_type=jnp.float32)

    live = layers_ref[lax.axis_index("section")] > slot
    write_live(live, g_ref, g_out_ref, [out], compute)


def general_layer(slot, span_order, section_layers, queries, gradient, saved_out, piece):
    tokens, width = gradient.shape
    kv_width = piece.shape[-1]
    groups = kv_width // DH
    repeat = width // kv_width
    keys_total = piece.shape[1]
    head_block = pl.BlockSpec((None, None, tokens, repeat * DH), lambda e: (0, slot, 0, e))
    grad_block = pl.BlockSpec((tokens, repeat * DH), lambda e: (0, e))
    key_block = pl.BlockSpec((2, keys_total, DH), lambda e: (0, 0, e))
    return pl.pallas_call(
        functools.partial(general_kernel, slot, repeat),
        grid=(groups,),
        in_specs=[
            pl.BlockSpec(memory_space=pltpu.SMEM),
            pl.BlockSpec(memory_space=pltpu.SMEM),
            head_block,
            grad_block,
            head_block,
            key_block,
        ],
        out_specs=[grad_block, key_block],
        out_shape=[
            jax.ShapeDtypeStruct((tokens, width), jnp.bfloat16),
            jax.ShapeDtypeStruct((2, keys_total, kv_width), jnp.float32),
        ],
        scratch_shapes=[pltpu.VMEM((keys_total, repeat * tokens), jnp.bfloat16)] * 2,
        compiler_params=pltpu.CompilerParams(vmem_limit_bytes=48 << 20),
        name=f"layer_{slot}",
    )(span_order, section_layers, queries, gradient, saved_out, piece)


def general_device(queries, keyvals, saved_out, grad_in, section_layers, span_order):
    slots = queries.shape[1]
    gradient = grad_in[0]
    results = [None] * slots
    for slot in reversed(range(slots)):
        piece = lax.all_gather(keyvals[0, slot], "ctx", axis=1, tiled=True)
        gradient, part = general_layer(
            slot, span_order, section_layers, queries, gradient, saved_out, piece
        )
        total = lax.psum_scatter(part, "ctx", scatter_dimension=1, tiled=True)
        results[slot] = total.astype(jnp.bfloat16)
    return jnp.stack(results)[None], shifted(gradient[None], "section", -1)


PARTS = (((0, 0), (0, 1)),) + tuple(((d, p),) for d in (1, 2, 3) for p in range(2))
TARGETS = (
    ((0, 0), (0, 1)),
    ((3, 0), (1, 0)),
    ((3, 1), (2, 1)),
    ((1, 1),),
    ((2, 0),),
)
TARGET_TYPES = (jnp.float32, jnp.bfloat16, jnp.bfloat16, jnp.float32, jnp.float32)


def square_layers(start, heads, span_order, section_layers, queries, gradient, saved_out, pieces):
    slots, tokens, width = queries.shape[1:]
    repeat = width // pieces[0].shape[-1]
    half = tokens // 2
    keys_total = span_order.shape[0] * half
    lanes = heads * DH
    at = start // heads
    head_block = pl.BlockSpec(
        (None, None, tokens, repeat * lanes), lambda s: (0, slots - 1 - s, 0, at)
    )
    own_block = pl.BlockSpec(
        (None, None, 2, tokens, lanes), lambda s: (0, slots - 1 - s, 0, 0, at)
    )
    return pl.pallas_call(
        functools.partial(square_kernel, PARTS, TARGETS, repeat, heads, slots),
        grid=(slots,),
        in_specs=[
            pl.BlockSpec(memory_space=pltpu.SMEM),
            pl.BlockSpec(memory_space=pltpu.SMEM),
            head_block,
            pl.BlockSpec((None, tokens, repeat * lanes), lambda s: (0, 0, at)),
            head_block,
            own_block,
        ]
        + [pl.BlockSpec((None, 2, half, lanes), lambda s: (slots - 1 - s, 0, 0, 0))] * 6,
        out_specs=[pl.BlockSpec((tokens, repeat * lanes), lambda s: (0, 0))]
        + [
            pl.BlockSpec((None, 2, len(parts) * half, lanes), lambda s: (slots - 1 - s, 0, 0, 0))
            for parts in TARGETS
        ],
        out_shape=[jax.ShapeDtypeStruct((tokens, repeat * lanes), jnp.bfloat16)]
        + [
            jax.ShapeDtypeStruct((slots, 2, len(parts) * half, lanes), dtype)
            for parts, dtype in zip(TARGETS, TARGET_TYPES)
        ],
        scratch_shapes=[
            pltpu.VMEM((tokens, repeat * lanes), jnp.bfloat16),
            pltpu.VMEM((heads, keys_total, DH), jnp.bfloat16),
            pltpu.VMEM((heads, keys_total, DH), jnp.bfloat16),
            pltpu.VMEM((heads, keys_total, DH), jnp.float32),
            pltpu.VMEM((heads, keys_total, DH), jnp.float32),
        ]
        + [
            pltpu.VMEM((heads, rows, repeat * half), jnp.bfloat16)
            for rows in (keys_total, keys_total // 2, keys_total, keys_total // 2)
        ],
        compiler_params=pltpu.CompilerParams(vmem_limit_bytes=48 << 20),
        cost_estimate=pl.CostEstimate(
            flops=10 * slots * tokens * repeat * lanes * keys_total,
            bytes_accessed=16 * slots * tokens * repeat * lanes,
            transcendentals=slots * tokens * repeat * heads * keys_total,
        ),
        name=f"layers_{start}",
    )(span_order, section_layers, queries, gradient, saved_out, *pieces)


CHUNKS = ((0, 2), (2, 4))


def on_device(queries, keyvals, saved_out, grad_in, section_layers, span_order):
    half = queries.shape[2] // 2
    if lax.axis_size("ctx") != 4 or keyvals.shape[4] != CHUNKS[-1][1] * DH:
        return general_device(queries, keyvals, saved_out, grad_in, section_layers, span_order)

    def gathered(start, stop):
        own = keyvals[0, :, :, :, start * DH : stop * DH]
        low = own[:, :, :half]
        high = own[:, :, half:]
        x_high = exchanged(high, "ctx", 1)
        y_low = exchanged(low, "ctx", 2)
        x_low = exchanged(low, "ctx", 1)
        y_high = exchanged(high, "ctx", 2)
        far_low = exchanged(y_low, "ctx", 1)
        far_high = exchanged(x_high, "ctx", 2)
        return [keyvals, x_low, x_high, y_low, y_high, far_low, far_high]

    def reduced(mine, first_x, first_y, rest_x, rest_y):
        got_x = exchanged(first_x, "ctx", 1)
        got_y = exchanged(first_y, "ctx", 2)
        second_x = (rest_x + got_y[:, :, :half].astype(jnp.float32)).astype(jnp.bfloat16)
        second_y = (rest_y + got_x[:, :, :half].astype(jnp.float32)).astype(jnp.bfloat16)
        more_x = exchanged(second_x, "ctx", 1)
        more_y = exchanged(second_y, "ctx", 2)
        low = (
            mine[:, :, :half]
            + got_x[:, :, half:].astype(jnp.float32)
            + more_y.astype(jnp.float32)
        )
        high = (
            mine[:, :, half:]
            + got_y[:, :, half:].astype(jnp.float32)
            + more_x.astype(jnp.float32)
        )
        return jnp.concatenate([low, high], axis=2).astype(jnp.bfloat16)

    pieces = [gathered(start, stop) for start, stop in CHUNKS]
    key_parts = []
    down_parts = []
    for (start, stop), own_pieces in zip(CHUNKS, pieces):
        gradient, *parts = square_layers(
            start, stop - start, span_order, section_layers, queries, grad_in, saved_out, own_pieces
        )
        down_parts.append(shifted(gradient, "section", -1))
        key_parts.append(reduced(*parts))
    grad_kv = jnp.concatenate(key_parts, axis=3)[None]
    grad_down = jnp.concatenate(down_parts, axis=1)[None]
    return (grad_kv, grad_down)


def solution(mesh):
    in_specs = (
        P("section", None, "ctx", None),
        P("section", None, None, "ctx", None),
        P("section", None, "ctx", None),
        P("section", "ctx", None),
        P(),
        P(),
    )
    out_specs = (P("section", None, None, "ctx", None), P("section", "ctx", None))
    return jax.shard_map(
        on_device, mesh=mesh, in_specs=in_specs, out_specs=out_specs, check_vma=False
    )
```

time: 66.2 us -> 55.8 us (0.84)
  the two profiles are of different devices: /device:TPU:9 before, /device:TPU:0 now
where the time goes in v2:
time: 55.8 us; the launch traced here: 55 us
  starting transfers between devices  33.6 us (60%)
  Pallas kernels  8.82 us (16%)
  waiting for transfers between devices  8.32 us (15%)
  other arithmetic  2.19 us (4%)
  local copies, waits for them, and re-layouts  1.23 us (2%)
  between operations  0.78 us (1%)
    ppermute x20, starting transfers between devices, exchanged(): return lax.ppermute(array, axis, [(i, i ^ mask) for i in range(length)])  25.6 us
    pallas_call x2, Pallas kernels, square_layers(): pl.pallas_call(functools.partial(square_kernel, PARTS, TARGETS, repeat, h...  8.82 us
    ppermute x20, waiting for transfers between devices, exchanged(): return lax.ppermute(array, axis, [(i, i ^ mask) for i in range(length)])  8.32 us
    ppermute x2, starting transfers between devices, shifted(): lax.ppermute(array, axis, [(i, (i + by) % length) for i in range(length)])  8.01 us
    squeeze x1, local copies, waits for them, and re-layouts, gathered(): own = keyvals[0, :, :, :, start * DH:stop * DH]  1.18 us
  transfers between devices with their start and end apart: 22, of which 7 were waited for; matrix products, arithmetic and copies ran while one was open for 2% of the time, Pallas kernels for 16%

profile of v2, /device:TPU:0, one launch (start us, length us, event | category | flops | bytes accessed | tf_op | source)
XLA Modules:
  0.0 55.0 jit_solution(11356434417852830203)
XLA Ops:
  0.7 1.2 %slice_bitcast_fusion.1 = (bf16[2,2,128,256]{3,2,1,0:T(8,128)(2,1)S(1)}, bf16[2,2,128,256]{3,2,1,0:T(8,128)(2,1)S(1)}) fusion(bf16[1,2,2,128,512]{4,3,2,1,0:T(8,128)(2,1)} %refs_0_.3), kind=kLoop, calls=%fused_computation.11 | loop fusion | bytes 1048576 | tf_op jit(solution)/shard_map/squeeze | solution.py:367
  1.9 3.0 %collective-permute-start.1 = (bf16[2,2,64,256]{3,2,1,0:T(8,128)(2,1)S(1)}, bf16[2,2,64,256]{3,2,1,0:T(8,128)(2,1)S(1)}, u32[]{:S(2)}, u32[]{:S(2)}) collective-permute-start(bf16[2,2,64,256]{3,2,1,0:T(8,128)(2,1)S(1)} %get-tuple-element.32), channel_id=1, source_target_pairs={{0,1},{1,0},{2,3},{3,2},{4,5},{5,4},{6,7},{7,6},{8,9},{9,8},{10,11... | collective-permute-start | bytes 393224 | tf_op jit(solution)/shard_map/ppermute | solution.py:18
  4.9 0.1 collective-permute-start.11
  5.0 2.0 %collective-permute-start.12 = (bf16[2,2,64,256]{3,2,1,0:T(8,128)(2,1)S(1)}, bf16[2,2,64,256]{3,2,1,0:T(8,128)(2,1)S(1)}, u32[]{:S(2)}, u32[]{:S(2)}) collective-permute-start(bf16[2,2,64,256]{3,2,1,0:T(8,128)(2,1)S(1)} %get-tuple-element.35), channel_id=1, source_target_pairs={{0,2},{1,3},{2,0},{3,1},{4,6},{5,7},{6,4},{7,5},{8,10},{9,11},{10,... | collective-permute-start | bytes 393224 | tf_op jit(solution)/shard_map/ppermute | solution.py:18
  7.0 0.1 collective-permute-start.2
  7.1 2.0 %collective-permute-start.13 = (bf16[2,2,64,256]{3,2,1,0:T(8,128)(2,1)S(1)}, bf16[2,2,64,256]{3,2,1,0:T(8,128)(2,1)S(1)}, u32[]{:S(2)}, u32[]{:S(2)}) collective-permute-start(bf16[2,2,64,256]{3,2,1,0:T(8,128)(2,1)S(1)} %get-tuple-element.34), channel_id=1, source_target_pairs={{0,2},{1,3},{2,0},{3,1},{4,6},{5,7},{6,4},{7,5},{8,10},{9,11},{10,... | collective-permute-start | bytes 393224 | tf_op jit(solution)/shard_map/ppermute | solution.py:18
  9.1 0.2 collective-permute-done.1.refs_2_
  9.2 2.1 %collective-permute-start.10 = (bf16[2,2,64,256]{3,2,1,0:T(8,128)(2,1)S(1)}, bf16[2,2,64,256]{3,2,1,0:T(8,128)(2,1)S(1)}, u32[]{:S(2)}, u32[]{:S(2)}) collective-permute-start(bf16[2,2,64,256]{3,2,1,0:T(8,128)(2,1)S(1)} %get-tuple-element.35), channel_id=1, source_target_pairs={{0,1},{1,0},{2,3},{3,2},{4,5},{5,4},{6,7},{7,6},{8,9},{9,8},{10,11... | collective-permute-start | bytes 393224 | tf_op jit(solution)/shard_map/ppermute | solution.py:18
  11.3 0.7 %collective-permute-done.11.refs_2_ = bf16[2,2,64,256]{3,2,1,0:T(8,128)(2,1)S(1)} collective-permute-done((bf16[2,2,64,256]{3,2,1,0:T(8,128)(2,1)S(1)}, bf16[2,2,64,256]{3,2,1,0:T(8,128)(2,1)S(1)}, u32[]{:S(2)}, u32[]{:S(2)}) %collective-permute-start.11) | collective-permute-done | bytes 131104 | tf_op jit(solution)/shard_map/ppermute | solution.py:18
  12.0 2.1 %collective-permute-start.15 = (bf16[2,2,64,256]{3,2,1,0:T(8,128)(2,1)S(1)}, bf16[2,2,64,256]{3,2,1,0:T(8,128)(2,1)S(1)}, u32[]{:S(2)}, u32[]{:S(2)}) collective-permute-start(bf16[2,2,64,256]{3,2,1,0:T(8,128)(2,1)S(1)} %collective-permute-done.11.refs_2_), channel_id=1, source_target_pairs={{0,2},{1,3},{2,0},{3,1},{4,6},{5,7},{6,4},{7,5},{8,10},{9,11},{10,... | collective-permute-start | bytes 393224 | tf_op jit(solution)/shard_map/ppermute | solution.py:18
  14.1 0.0 collective-permute-done.12.refs_3_
  14.1 1.5 %collective-permute-start.14 = (bf16[2,2,64,256]{3,2,1,0:T(8,128)(2,1)S(1)}, bf16[2,2,64,256]{3,2,1,0:T(8,128)(2,1)S(1)}, u32[]{:S(2)}, u32[]{:S(2)}) collective-permute-start(bf16[2,2,64,256]{3,2,1,0:T(8,128)(2,1)S(1)} %collective-permute-done.12.refs_3_), channel_id=1, source_target_pairs={{0,1},{1,0},{2,3},{3,2},{4,5},{5,4},{6,7},{7,6},{8,9},{9,8},{10,11... | collective-permute-start | bytes 393224 | tf_op jit(solution)/shard_map/ppermute | solution.py:18
  15.6 0.0 collective-permute-done.2.refs_3_
  15.6 0.7 %collective-permute-start.3 = (bf16[2,2,64,256]{3,2,1,0:T(8,128)(2,1)S(1)}, bf16[2,2,64,256]{3,2,1,0:T(8,128)(2,1)S(1)}, u32[]{:S(2)}, u32[]{:S(2)}) collective-permute-start(bf16[2,2,64,256]{3,2,1,0:T(8,128)(2,1)S(1)} %get-tuple-element.32), channel_id=1, source_target_pairs={{0,2},{1,3},{2,0},{3,1},{4,6},{5,7},{6,4},{7,5},{8,10},{9,11},{10,... | collective-permute-start | bytes 393224 | tf_op jit(solution)/shard_map/ppermute | solution.py:18
  16.3 0.8 %collective-permute-done.13.refs_4_ = bf16[2,2,64,256]{3,2,1,0:T(8,128)(2,1)S(1)} collective-permute-done((bf16[2,2,64,256]{3,2,1,0:T(8,128)(2,1)S(1)}, bf16[2,2,64,256]{3,2,1,0:T(8,128)(2,1)S(1)}, u32[]{:S(2)}, u32[]{:S(2)}) %collective-permute-start.13) | collective-permute-done | bytes 131104 | tf_op jit(solution)/shard_map/ppermute | solution.py:18
  17.0 2.0 %collective-permute-start = (bf16[2,2,64,256]{3,2,1,0:T(8,128)(2,1)S(1)}, bf16[2,2,64,256]{3,2,1,0:T(8,128)(2,1)S(1)}, u32[]{:S(2)}, u32[]{:S(2)}) collective-permute-start(bf16[2,2,64,256]{3,2,1,0:T(8,128)(2,1)S(1)} %get-tuple-element.33), channel_id=1, source_target_pairs={{0,1},{1,0},{2,3},{3,2},{4,5},{5,4},{6,7},{7,6},{8,9},{9,8},{10,11... | collective-permute-start | bytes 393224 | tf_op jit(solution)/shard_map/ppermute | solution.py:18
  19.1 0.0 collective-permute-done.10.refs_1_
  19.1 1.5 %collective-permute-start.5 = (bf16[2,2,64,256]{3,2,1,0:T(8,128)(2,1)S(1)}, bf16[2,2,64,256]{3,2,1,0:T(8,128)(2,1)S(1)}, u32[]{:S(2)}, u32[]{:S(2)}) collective-permute-start(bf16[2,2,64,256]{3,2,1,0:T(8,128)(2,1)S(1)} %collective-permute-done.1.refs_2_), channel_id=1, source_target_pairs={{0,2},{1,3},{2,0},{3,1},{4,6},{5,7},{6,4},{7,5},{8,10},{9,11},{10,... | collective-permute-start | bytes 393224 | tf_op jit(solution)/shard_map/ppermute | solution.py:18
  20.6 0.0 collective-permute-done.15.refs_6_
  20.6 1.3 %collective-permute-start.4 = (bf16[2,2,64,256]{3,2,1,0:T(8,128)(2,1)S(1)}, bf16[2,2,64,256]{3,2,1,0:T(8,128)(2,1)S(1)}, u32[]{:S(2)}, u32[]{:S(2)}) collective-permute-start(bf16[2,2,64,256]{3,2,1,0:T(8,128)(2,1)S(1)} %collective-permute-done.2.refs_3_), channel_id=1, source_target_pairs={{0,1},{1,0},{2,3},{3,2},{4,5},{5,4},{6,7},{7,6},{8,9},{9,8},{10,11... | collective-permute-start | bytes 393224 | tf_op jit(solution)/shard_map/ppermute | solution.py:18
  21.9 0.0 collective-permute-done.14.refs_5_
  21.9 4.4 %layers_2.1 = (bf16[128,2048]{1,0:T(8,128)(2,1)S(1)}, f32[2,2,128,256]{3,2,1,0:T(8,128)S(1)}, bf16[2,2,128,256]{3,2,1,0:T(8,128)(2,1)S(1)}, bf16[2,2,128,256]{3,...) custom-call(s32[8]{0:T(128)S(1)} %copy-done.2, s32[8]{0:T(128)S(1)} %copy-done.3, ...), custom_call_target="tpu_custom_call" | custom-call | flops 2684354560 | bytes 8388608 | tf_op jit(solution)/shard_map/layers_2/pallas_call | solution.py:315
  26.3 0.7 %collective-permute-start.16 = (bf16[2,2,128,256]{3,2,1,0:T(8,128)(2,1)S(1)}, bf16[2,2,128,256]{3,2,1,0:T(8,128)(2,1)S(1)}, u32[]{:S(2)}, u32[]{:S(2)}) collective-permute-start(bf16[2,2,128,256]{3,2,1,0:T(8,128)(2,1)S(1)} %get-tuple-element.20), channel_id=1, source_target_pairs={{0,1},{1,0},{2,3},{3,2},{4,5},{5,4},{6,7},{7,6},{8,9},{9,8},{10,11... | collective-permute-start | bytes 786440 | tf_op jit(solution)/shard_map/ppermute | solution.py:18
  27.0 0.0 collective-permute-done.3.refs_4_
  27.0 1.4 %collective-permute-start.18 = (bf16[2,2,128,256]{3,2,1,0:T(8,128)(2,1)S(1)}, bf16[2,2,128,256]{3,2,1,0:T(8,128)(2,1)S(1)}, u32[]{:S(2)}, u32[]{:S(2)}) collective-permute-start(bf16[2,2,128,256]{3,2,1,0:T(8,128)(2,1)S(1)} %get-tuple-element.22), channel_id=1, source_target_pairs={{0,2},{1,3},{2,0},{3,1},{4,6},{5,7},{6,4},{7,5},{8,10},{9,11},{10,... | collective-permute-start | bytes 786440 | tf_op jit(solution)/shard_map/ppermute | solution.py:18
  28.4 0.0 collective-permute-done.refs_1_
  28.4 1.4 %collective-permute-start.21 = (bf16[128,2048]{1,0:T(8,128)(2,1)S(1)}, bf16[128,2048]{1,0:T(8,128)(2,1)S(1)}, u32[]{:S(2)}, u32[]{:S(2)}) collective-permute-start(bf16[128,2048]{1,0:T(8,128)(2,1)S(1)} %get-tuple-element.25), channel_id=1, source_target_pairs={{0,28},{4,0},{8,4},{12,8},{16,12},{20,16},{24,20},{28,24},{1,29},{... | collective-permute-start | bytes 1572872 | tf_op jit(solution)/shard_map/ppermute | solution.py:23
  29.8 0.0 collective-permute-done.5.refs_6_
  29.8 0.0 collective-permute-done.4.refs_5_
  29.8 4.4 %layers_0.1 = (bf16[128,2048]{1,0:T(8,128)(2,1)S(1)}, f32[2,2,128,256]{3,2,1,0:T(8,128)S(1)}, bf16[2,2,128,256]{3,2,1,0:T(8,128)(2,1)S(1)}, bf16[2,2,128,256]{3,...) custom-call(s32[8]{0:T(128)S(1)} %copy-done.2, s32[8]{0:T(128)S(1)} %copy-done.3, ...), custom_call_target="tpu_custom_call" | custom-call | flops 2684354560 | bytes 8388608 | tf_op jit(solution)/shard_map/layers_0/pallas_call | solution.py:315
  34.2 1.4 %collective-permute-start.6 = (bf16[2,2,128,256]{3,2,1,0:T(8,128)(2,1)S(1)}, bf16[2,2,128,256]{3,2,1,0:T(8,128)(2,1)S(1)}, u32[]{:S(2)}, u32[]{:S(2)}) collective-permute-start(bf16[2,2,128,256]{3,2,1,0:T(8,128)(2,1)S(1)} %get-tuple-element.15), channel_id=1, source_target_pairs={{0,1},{1,0},{2,3},{3,2},{4,5},{5,4},{6,7},{7,6},{8,9},{9,8},{10,11... | collective-permute-start | bytes 786440 | tf_op jit(solution)/shard_map/ppermute | solution.py:18
  35.6 0.7 %collective-permute-start.8 = (bf16[2,2,128,256]{3,2,1,0:T(8,128)(2,1)S(1)}, bf16[2,2,128,256]{3,2,1,0:T(8,128)(2,1)S(1)}, u32[]{:S(2)}, u32[]{:S(2)}) collective-permute-start(bf16[2,2,128,256]{3,2,1,0:T(8,128)(2,1)S(1)} %get-tuple-element.17), channel_id=1, source_target_pairs={{0,2},{1,3},{2,0},{3,1},{4,6},{5,7},{6,4},{7,5},{8,10},{9,11},{10,... | collective-permute-start | bytes 786440 | tf_op jit(solution)/shard_map/ppermute | solution.py:18
  36.3 0.0 collective-permute-done.16
  36.3 6.6 %collective-permute-start.20 = (bf16[128,2048]{1,0:T(8,128)(2,1)S(1)}, bf16[128,2048]{1,0:T(8,128)(2,1)S(1)}, u32[]{:S(2)}, u32[]{:S(2)}) collective-permute-start(bf16[128,2048]{1,0:T(8,128)(2,1)S(1)} %get-tuple-element.24), channel_id=1, source_target_pairs={{0,28},{4,0},{8,4},{12,8},{16,12},{20,16},{24,20},{28,24},{1,29},{... | collective-permute-start | bytes 1572872 | tf_op jit(solution)/shard_map/ppermute | solution.py:23
  43.0 1.3 %collective-permute-start.17 = (bf16[2,2,64,256]{3,2,1,0:T(8,128)(2,1)S(1)}, bf16[2,2,64,256]{3,2,1,0:T(8,128)(2,1)S(1)}, u32[]{:S(2)}, u32[]{:S(2)}) collective-permute-start(bf16[2,2,64,256]{3,2,1,0:T(8,128)(2,1)S(1)} %add_convert_fusion.3), channel_id=1, source_target_pairs={{0,2},{1,3},{2,0},{3,1},{4,6},{5,7},{6,4},{7,5},{8,10},{9,11},{10,... | collective-permute-start | bytes 393224 | tf_op jit(solution)/shard_map/ppermute | solution.py:18
  44.3 0.0 collective-permute-done.6
  44.3 0.9 %collective-permute-start.19 = (bf16[2,2,64,256]{3,2,1,0:T(8,128)(2,1)S(1)}, bf16[2,2,64,256]{3,2,1,0:T(8,128)(2,1)S(1)}, u32[]{:S(2)}, u32[]{:S(2)}) collective-permute-start(bf16[2,2,64,256]{3,2,1,0:T(8,128)(2,1)S(1)} %add_convert_fusion.1), channel_id=1, source_target_pairs={{0,1},{1,0},{2,3},{3,2},{4,5},{5,4},{6,7},{7,6},{8,9},{9,8},{10,11... | collective-permute-start | bytes 393224 | tf_op jit(solution)/shard_map/ppermute | solution.py:18
  45.3 0.0 collective-permute-done.8
  45.3 0.5 collective-permute-start.7
  45.8 2.2 %collective-permute-done.17 = bf16[2,2,64,256]{3,2,1,0:T(8,128)(2,1)S(1)} collective-permute-done((bf16[2,2,64,256]{3,2,1,0:T(8,128)(2,1)S(1)}, bf16[2,2,64,256]{3,2,1,0:T(8,128)(2,1)S(1)}, u32[]{:S(2)}, u32[]{:S(2)}) %collective-permute-start.17) | collective-permute-done | bytes 131104 | tf_op jit(solution)/shard_map/ppermute | solution.py:18
  48.0 0.5 collective-permute-start.9
  48.5 0.9 %collective-permute-done.19 = bf16[2,2,64,256]{3,2,1,0:T(8,128)(2,1)S(1)} collective-permute-done((bf16[2,2,64,256]{3,2,1,0:T(8,128)(2,1)S(1)}, bf16[2,2,64,256]{3,2,1,0:T(8,128)(2,1)S(1)}, u32[]{:S(2)}, u32[]{:S(2)}) %collective-permute-start.19) | collective-permute-done | bytes 131104 | tf_op jit(solution)/shard_map/ppermute | solution.py:18
  49.4 0.1 add_convert_fusion.2
  49.5 0.8 %collective-permute-done.7 = bf16[2,2,64,256]{3,2,1,0:T(8,128)(2,1)S(1)} collective-permute-done((bf16[2,2,64,256]{3,2,1,0:T(8,128)(2,1)S(1)}, bf16[2,2,64,256]{3,2,1,0:T(8,128)(2,1)S(1)}, u32[]{:S(2)}, u32[]{:S(2)}) %collective-permute-start.7) | collective-permute-done | bytes 131104 | tf_op jit(solution)/shard_map/ppermute | solution.py:18
  50.3 2.7 %collective-permute-done.9 = bf16[2,2,64,256]{3,2,1,0:T(8,128)(2,1)S(1)} collective-permute-done((bf16[2,2,64,256]{3,2,1,0:T(8,128)(2,1)S(1)}, bf16[2,2,64,256]{3,2,1,0:T(8,128)(2,1)S(1)}, u32[]{:S(2)}, u32[]{:S(2)}) %collective-permute-start.9) | collective-permute-done | bytes 131104 | tf_op jit(solution)/shard_map/ppermute | solution.py:18
  53.0 0.1 add_convert_fusion.6
  53.1 0.8 %maximum_bitcast_fusion.1 = bf16[1,2,2,128,512]{4,3,2,1,0:T(8,128)(2,1)} fusion(bf16[2,2,64,256]{3,2,1,0:T(8,128)(2,1)S(1)} %get-tuple-element.31, bf16[2,2,64,256]{3,2,1,0:T(8,128)(2,1)S(1)} %get-tuple-element.30, bf16[2,2,64,256]{3,2,1,0:T(8,128)(2,1)S(1)} %get-tuple-element.27, bf16[2,2,64,256]{3,2,1,0:T(8,128)(2,1)S(1)} %get-tuple-element.26), kind=kLoop, calls=%fused_computation.1 | loop fusion | flops 2097152 | bytes 1048576 | tf_op jit(solution)/shard_map/broadcast_in_dim | solution.py:406
  53.9 1.0 %maximum_bitcast_fusion = bf16[1,128,4096]{2,1,0:T(8,128)(2,1)} fusion(bf16[128,2048]{1,0:T(8,128)(2,1)S(1)} %collective-permute-done.21, bf16[128,2048]{1,0:T(8,128)(2,1)S(1)} %collective-permute-done.20), kind=kLoop, calls=%fused_computation | loop fusion | flops 2097152 | bytes 2097152 | tf_op jit(solution)/shard_map/broadcast_in_dim | solution.py:407
  (17 shorter events, 0.2 us)
Async XLA Ops:
  0.6 21.2 %copy-start = (bf16[1,2,2,128,512]{4,3,2,1,0:T(8,128)(2,1)S(1)}, bf16[1,2,2,128,512]{4,3,2,1,0:T(8,128)(2,1)}, u32[]{:S(2)}) copy-start(bf16[1,2,2,128,512]{4,3,2,1,0:T(8,128)(2,1)} %refs_0_.3) | copy-start | bytes 1572868
  0.6 21.2 %copy-start.2 = (s32[8]{0:T(128)S(1)}, s32[8]{0:T(128)}, u32[]{:S(2)}) copy-start(s32[8]{0:T(128)} %spans_ref.3) | copy-start | bytes 100
  0.7 21.2 %copy-start.3 = (s32[8]{0:T(128)S(1)}, s32[8]{0:T(128)}, u32[]{:S(2)}) copy-start(s32[8]{0:T(128)} %layers_ref.3) | copy-start | bytes 100
  0.7 21.2 %copy-start.1 = (bf16[1,128,4096]{2,1,0:T(8,128)(2,1)S(1)}, bf16[1,128,4096]{2,1,0:T(8,128)(2,1)}, u32[]{:S(2)}) copy-start(bf16[1,128,4096]{2,1,0:T(8,128)(2,1)} %g_ref.3) | copy-start | bytes 3145732
  1.9 7.3 %collective-permute-start.1 = (bf16[2,2,64,256]{3,2,1,0:T(8,128)(2,1)S(1)}, bf16[2,2,64,256]{3,2,1,0:T(8,128)(2,1)S(1)}, u32[]{:S(2)}, u32[]{:S(2)}) collective-permute-start(bf16[2,2,64,256]{3,2,1,0:T(8,128)(2,1)S(1)} %get-tuple-element.32), channel_id=1, source_target_pairs={{0,1},{1,0},{2,3},{3,2},{4,5},{5,4},{6,7},{7,6},{8,9},{9,8},{10,11... | collective-permute-start | bytes 393224 | tf_op jit(solution)/shard_map/ppermute | solution.py:18
  4.9 7.1 %collective-permute-start.11 = (bf16[2,2,64,256]{3,2,1,0:T(8,128)(2,1)S(1)}, bf16[2,2,64,256]{3,2,1,0:T(8,128)(2,1)S(1)}, u32[]{:S(2)}, u32[]{:S(2)}) collective-permute-start(bf16[2,2,64,256]{3,2,1,0:T(8,128)(2,1)S(1)} %get-tuple-element.34), channel_id=1, source_target_pairs={{0,1},{1,0},{2,3},{3,2},{4,5},{5,4},{6,7},{7,6},{8,9},{9,8},{10,11... | collective-permute-start | bytes 393224 | tf_op jit(solution)/shard_map/ppermute | solution.py:18
  5.0 9.1 %collective-permute-start.12 = (bf16[2,2,64,256]{3,2,1,0:T(8,128)(2,1)S(1)}, bf16[2,2,64,256]{3,2,1,0:T(8,128)(2,1)S(1)}, u32[]{:S(2)}, u32[]{:S(2)}) collective-permute-start(bf16[2,2,64,256]{3,2,1,0:T(8,128)(2,1)S(1)} %get-tuple-element.35), channel_id=1, source_target_pairs={{0,2},{1,3},{2,0},{3,1},{4,6},{5,7},{6,4},{7,5},{8,10},{9,11},{10,... | collective-permute-start | bytes 393224 | tf_op jit(solution)/shard_map/ppermute | solution.py:18
  7.0 8.6 %collective-permute-start.2 = (bf16[2,2,64,256]{3,2,1,0:T(8,128)(2,1)S(1)}, bf16[2,2,64,256]{3,2,1,0:T(8,128)(2,1)S(1)}, u32[]{:S(2)}, u32[]{:S(2)}) collective-permute-start(bf16[2,2,64,256]{3,2,1,0:T(8,128)(2,1)S(1)} %get-tuple-element.33), channel_id=1, source_target_pairs={{0,2},{1,3},{2,0},{3,1},{4,6},{5,7},{6,4},{7,5},{8,10},{9,11},{10,... | collective-permute-start | bytes 393224 | tf_op jit(solution)/shard_map/ppermute | solution.py:18
  7.1 10.0 %collective-permute-start.13 = (bf16[2,2,64,256]{3,2,1,0:T(8,128)(2,1)S(1)}, bf16[2,2,64,256]{3,2,1,0:T(8,128)(2,1)S(1)}, u32[]{:S(2)}, u32[]{:S(2)}) collective-permute-start(bf16[2,2,64,256]{3,2,1,0:T(8,128)(2,1)S(1)} %get-tuple-element.34), channel_id=1, source_target_pairs={{0,2},{1,3},{2,0},{3,1},{4,6},{5,7},{6,4},{7,5},{8,10},{9,11},{10,... | collective-permute-start | bytes 393224 | tf_op jit(solution)/shard_map/ppermute | solution.py:18
  9.2 9.8 %collective-permute-start.10 = (bf16[2,2,64,256]{3,2,1,0:T(8,128)(2,1)S(1)}, bf16[2,2,64,256]{3,2,1,0:T(8,128)(2,1)S(1)}, u32[]{:S(2)}, u32[]{:S(2)}) collective-permute-start(bf16[2,2,64,256]{3,2,1,0:T(8,128)(2,1)S(1)} %get-tuple-element.35), channel_id=1, source_target_pairs={{0,1},{1,0},{2,3},{3,2},{4,5},{5,4},{6,7},{7,6},{8,9},{9,8},{10,11... | collective-permute-start | bytes 393224 | tf_op jit(solution)/shard_map/ppermute | solution.py:18
  12.0 8.6 %collective-permute-start.15 = (bf16[2,2,64,256]{3,2,1,0:T(8,128)(2,1)S(1)}, bf16[2,2,64,256]{3,2,1,0:T(8,128)(2,1)S(1)}, u32[]{:S(2)}, u32[]{:S(2)}) collective-permute-start(bf16[2,2,64,256]{3,2,1,0:T(8,128)(2,1)S(1)} %collective-permute-done.11.refs_2_), channel_id=1, source_target_pairs={{0,2},{1,3},{2,0},{3,1},{4,6},{5,7},{6,4},{7,5},{8,10},{9,11},{10,... | collective-permute-start | bytes 393224 | tf_op jit(solution)/shard_map/ppermute | solution.py:18
  14.1 7.8 %collective-permute-start.14 = (bf16[2,2,64,256]{3,2,1,0:T(8,128)(2,1)S(1)}, bf16[2,2,64,256]{3,2,1,0:T(8,128)(2,1)S(1)}, u32[]{:S(2)}, u32[]{:S(2)}) collective-permute-start(bf16[2,2,64,256]{3,2,1,0:T(8,128)(2,1)S(1)} %collective-permute-done.12.refs_3_), channel_id=1, source_target_pairs={{0,1},{1,0},{2,3},{3,2},{4,5},{5,4},{6,7},{7,6},{8,9},{9,8},{10,11... | collective-permute-start | bytes 393224 | tf_op jit(solution)/shard_map/ppermute | solution.py:18
  15.6 11.4 %collective-permute-start.3 = (bf16[2,2,64,256]{3,2,1,0:T(8,128)(2,1)S(1)}, bf16[2,2,64,256]{3,2,1,0:T(8,128)(2,1)S(1)}, u32[]{:S(2)}, u32[]{:S(2)}) collective-permute-start(bf16[2,2,64,256]{3,2,1,0:T(8,128)(2,1)S(1)} %get-tuple-element.32), channel_id=1, source_target_pairs={{0,2},{1,3},{2,0},{3,1},{4,6},{5,7},{6,4},{7,5},{8,10},{9,11},{10,... | collective-permute-start | bytes 393224 | tf_op jit(solution)/shard_map/ppermute | solution.py:18
  17.0 11.3 %collective-permute-start = (bf16[2,2,64,256]{3,2,1,0:T(8,128)(2,1)S(1)}, bf16[2,2,64,256]{3,2,1,0:T(8,128)(2,1)S(1)}, u32[]{:S(2)}, u32[]{:S(2)}) collective-permute-start(bf16[2,2,64,256]{3,2,1,0:T(8,128)(2,1)S(1)} %get-tuple-element.33), channel_id=1, source_target_pairs={{0,1},{1,0},{2,3},{3,2},{4,5},{5,4},{6,7},{7,6},{8,9},{9,8},{10,11... | collective-permute-start | bytes 393224 | tf_op jit(solution)/shard_map/ppermute | solution.py:18
  19.1 10.7 %collective-permute-start.5 = (bf16[2,2,64,256]{3,2,1,0:T(8,128)(2,1)S(1)}, bf16[2,2,64,256]{3,2,1,0:T(8,128)(2,1)S(1)}, u32[]{:S(2)}, u32[]{:S(2)}) collective-permute-start(bf16[2,2,64,256]{3,2,1,0:T(8,128)(2,1)S(1)} %collective-permute-done.1.refs_2_), channel_id=1, source_target_pairs={{0,2},{1,3},{2,0},{3,1},{4,6},{5,7},{6,4},{7,5},{8,10},{9,11},{10,... | collective-permute-start | bytes 393224 | tf_op jit(solution)/shard_map/ppermute | solution.py:18
  20.6 9.2 %collective-permute-start.4 = (bf16[2,2,64,256]{3,2,1,0:T(8,128)(2,1)S(1)}, bf16[2,2,64,256]{3,2,1,0:T(8,128)(2,1)S(1)}, u32[]{:S(2)}, u32[]{:S(2)}) collective-permute-start(bf16[2,2,64,256]{3,2,1,0:T(8,128)(2,1)S(1)} %collective-permute-done.2.refs_3_), channel_id=1, source_target_pairs={{0,1},{1,0},{2,3},{3,2},{4,5},{5,4},{6,7},{7,6},{8,9},{9,8},{10,11... | collective-permute-start | bytes 393224 | tf_op jit(solution)/shard_map/ppermute | solution.py:18
  26.3 10.0 %collective-permute-start.16 = (bf16[2,2,128,256]{3,2,1,0:T(8,128)(2,1)S(1)}, bf16[2,2,128,256]{3,2,1,0:T(8,128)(2,1)S(1)}, u32[]{:S(2)}, u32[]{:S(2)}) collective-permute-start(bf16[2,2,128,256]{3,2,1,0:T(8,128)(2,1)S(1)} %get-tuple-element.20), channel_id=1, source_target_pairs={{0,1},{1,0},{2,3},{3,2},{4,5},{5,4},{6,7},{7,6},{8,9},{9,8},{10,11... | collective-permute-start | bytes 786440 | tf_op jit(solution)/shard_map/ppermute | solution.py:18
  27.0 16.0 %collective-permute-start.18 = (bf16[2,2,128,256]{3,2,1,0:T(8,128)(2,1)S(1)}, bf16[2,2,128,256]{3,2,1,0:T(8,128)(2,1)S(1)}, u32[]{:S(2)}, u32[]{:S(2)}) collective-permute-start(bf16[2,2,128,256]{3,2,1,0:T(8,128)(2,1)S(1)} %get-tuple-element.22), channel_id=1, source_target_pairs={{0,2},{1,3},{2,0},{3,1},{4,6},{5,7},{6,4},{7,5},{8,10},{9,11},{10,... | collective-permute-start | bytes 786440 | tf_op jit(solution)/shard_map/ppermute | solution.py:18
  28.4 25.6 %collective-permute-start.21 = (bf16[128,2048]{1,0:T(8,128)(2,1)S(1)}, bf16[128,2048]{1,0:T(8,128)(2,1)S(1)}, u32[]{:S(2)}, u32[]{:S(2)}) collective-permute-start(bf16[128,2048]{1,0:T(8,128)(2,1)S(1)} %get-tuple-element.25), channel_id=1, source_target_pairs={{0,28},{4,0},{8,4},{12,8},{16,12},{20,16},{24,20},{28,24},{1,29},{... | collective-permute-start | bytes 1572872 | tf_op jit(solution)/shard_map/ppermute | solution.py:23
  34.2 10.2 %collective-permute-start.6 = (bf16[2,2,128,256]{3,2,1,0:T(8,128)(2,1)S(1)}, bf16[2,2,128,256]{3,2,1,0:T(8,128)(2,1)S(1)}, u32[]{:S(2)}, u32[]{:S(2)}) collective-permute-start(bf16[2,2,128,256]{3,2,1,0:T(8,128)(2,1)S(1)} %get-tuple-element.15), channel_id=1, source_target_pairs={{0,1},{1,0},{2,3},{3,2},{4,5},{5,4},{6,7},{7,6},{8,9},{9,8},{10,11... | collective-permute-start | bytes 786440 | tf_op jit(solution)/shard_map/ppermute | solution.py:18
  35.6 9.7 %collective-permute-start.8 = (bf16[2,2,128,256]{3,2,1,0:T(8,128)(2,1)S(1)}, bf16[2,2,128,256]{3,2,1,0:T(8,128)(2,1)S(1)}, u32[]{:S(2)}, u32[]{:S(2)}) collective-permute-start(bf16[2,2,128,256]{3,2,1,0:T(8,128)(2,1)S(1)} %get-tuple-element.17), channel_id=1, source_target_pairs={{0,2},{1,3},{2,0},{3,1},{4,6},{5,7},{6,4},{7,5},{8,10},{9,11},{10,... | collective-permute-start | bytes 786440 | tf_op jit(solution)/shard_map/ppermute | solution.py:18
  36.3 17.6 %collective-permute-start.20 = (bf16[128,2048]{1,0:T(8,128)(2,1)S(1)}, bf16[128,2048]{1,0:T(8,128)(2,1)S(1)}, u32[]{:S(2)}, u32[]{:S(2)}) collective-permute-start(bf16[128,2048]{1,0:T(8,128)(2,1)S(1)} %get-tuple-element.24), channel_id=1, source_target_pairs={{0,28},{4,0},{8,4},{12,8},{16,12},{20,16},{24,20},{28,24},{1,29},{... | collective-permute-start | bytes 1572872 | tf_op jit(solution)/shard_map/ppermute | solution.py:23
  43.0 5.0 %collective-permute-start.17 = (bf16[2,2,64,256]{3,2,1,0:T(8,128)(2,1)S(1)}, bf16[2,2,64,256]{3,2,1,0:T(8,128)(2,1)S(1)}, u32[]{:S(2)}, u32[]{:S(2)}) collective-permute-start(bf16[2,2,64,256]{3,2,1,0:T(8,128)(2,1)S(1)} %add_convert_fusion.3), channel_id=1, source_target_pairs={{0,2},{1,3},{2,0},{3,1},{4,6},{5,7},{6,4},{7,5},{8,10},{9,11},{10,... | collective-permute-start | bytes 393224 | tf_op jit(solution)/shard_map/ppermute | solution.py:18
  44.3 5.0 %collective-permute-start.19 = (bf16[2,2,64,256]{3,2,1,0:T(8,128)(2,1)S(1)}, bf16[2,2,64,256]{3,2,1,0:T(8,128)(2,1)S(1)}, u32[]{:S(2)}, u32[]{:S(2)}) collective-permute-start(bf16[2,2,64,256]{3,2,1,0:T(8,128)(2,1)S(1)} %add_convert_fusion.1), channel_id=1, source_target_pairs={{0,1},{1,0},{2,3},{3,2},{4,5},{5,4},{6,7},{7,6},{8,9},{9,8},{10,11... | collective-permute-start | bytes 393224 | tf_op jit(solution)/shard_map/ppermute | solution.py:18
  45.3 5.0 %collective-permute-start.7 = (bf16[2,2,64,256]{3,2,1,0:T(8,128)(2,1)S(1)}, bf16[2,2,64,256]{3,2,1,0:T(8,128)(2,1)S(1)}, u32[]{:S(2)}, u32[]{:S(2)}) collective-permute-start(bf16[2,2,64,256]{3,2,1,0:T(8,128)(2,1)S(1)} %add_convert_fusion.7), channel_id=1, source_target_pairs={{0,2},{1,3},{2,0},{3,1},{4,6},{5,7},{6,4},{7,5},{8,10},{9,11},{10,... | collective-permute-start | bytes 393224 | tf_op jit(solution)/shard_map/ppermute | solution.py:18
  48.0 5.0 %collective-permute-start.9 = (bf16[2,2,64,256]{3,2,1,0:T(8,128)(2,1)S(1)}, bf16[2,2,64,256]{3,2,1,0:T(8,128)(2,1)S(1)}, u32[]{:S(2)}, u32[]{:S(2)}) collective-permute-start(bf16[2,2,64,256]{3,2,1,0:T(8,128)(2,1)S(1)} %add_convert_fusion.5), channel_id=1, source_target_pairs={{0,1},{1,0},{2,3},{3,2},{4,5},{5,4},{6,7},{7,6},{8,9},{9,8},{10,11... | collective-permute-start | bytes 393224 | tf_op jit(solution)/shard_map/ppermute | solution.py:18

commit v3 on v2

--- a/solution.py
+++ b/solution.py
@@ -46,13 +46,13 @@
     return (powers * inverse).astype(jnp.bfloat16)
 
 
-def square_kernel(parts_of, targets, repeat, heads, slots, spans_ref, layers_ref, q_ref, g_ref, o_ref, *refs):
+def square_kernel(parts_of, targets, repeat, heads, slots, meta_ref, q_ref, g_ref, o_ref, *refs):
     pieces = refs[: len(parts_of)]
     g_out_ref = refs[len(parts_of)]
     outs = refs[len(parts_of) + 1 : len(parts_of) + 1 + len(targets)]
     g_s, k_s, v_s, dk_s, dv_s, p_hi, p_lo, ds_hi, ds_lo = refs[-9:]
     step = pl.program_id(0)
-    live = layers_ref[lax.axis_index("section")] > slots - 1 - step
+    live = meta_ref[k_s.shape[1] // (q_ref.shape[0] // 2) + lax.axis_index("section")] > slots - 1 - step
     span_rows = q_ref.shape[0] // 2
     spans = k_s.shape[1] // span_rows
     scale = DH ** (-0.5)
@@ -67,7 +67,7 @@
         g_s[...] = g_out_ref[...]
 
     def span_at(part):
-        return spans_ref[2 * (own ^ part[0]) + part[1]]
+        return meta_ref[2 * (own ^ part[0]) + part[1]]
 
     def rows_of(index):
         return pl.ds(pl.multiple_of(index * span_rows, span_rows), span_rows)
@@ -80,7 +80,7 @@
                     here = (slice(at * span_rows, (at + 1) * span_rows), slice(e * DH, (e + 1) * DH))
                     k_s[e, rows] = piece[(0, *here)]
                     v_s[e, rows] = piece[(1, *here)]
-        first, second = spans_ref[2 * own], spans_ref[2 * own + 1]
+        first, second = meta_ref[2 * own], meta_ref[2 * own + 1]
         low_span = jnp.minimum(first, second)
         high_part = (second > first).astype(jnp.int32)
 
@@ -288,51 +288,45 @@
     return jnp.stack(results)[None], shifted(gradient[None], "section", -1)
 
 
-PARTS = (((0, 0), (0, 1)),) + tuple(((d, p),) for d in (1, 2, 3) for p in range(2))
-TARGETS = (
-    ((0, 0), (0, 1)),
-    ((3, 0), (1, 0)),
-    ((3, 1), (2, 1)),
-    ((1, 1),),
-    ((2, 0),),
-)
-TARGET_TYPES = (jnp.float32, jnp.bfloat16, jnp.bfloat16, jnp.float32, jnp.float32)
-
-
-def square_layers(start, heads, span_order, section_layers, queries, gradient, saved_out, pieces):
+WHOLES = tuple(((d, 0), (d, 1)) for d in range(4))
+FULLS = (*WHOLES[:3], ((3, 0),), ((3, 1),))
+HALVES = (WHOLES[0],) + tuple(((d, p),) for d in (1, 2, 3) for p in range(2))
+TWO_PHASES = (WHOLES[0], ((3, 0), (1, 0)), ((3, 1), (2, 1)), ((1, 1),), ((2, 0),))
+FLOAT, SHORT = jnp.float32, jnp.bfloat16
+
+
+def square_layers(start, heads, meta, queries, gradient, saved_out, pieces, parts_of, targets, types):
     slots, tokens, width = queries.shape[1:]
-    repeat = width // pieces[0].shape[-1]
+    repeat = width // (CHUNKS[-1][1] * DH)
     half = tokens // 2
-    keys_total = span_order.shape[0] * half
+    keys_total = sum(len(parts) for parts in parts_of) * half
     lanes = heads * DH
     at = start // heads
     head_block = pl.BlockSpec(
         (None, None, tokens, repeat * lanes), lambda s: (0, slots - 1 - s, 0, at)
     )
-    own_block = pl.BlockSpec(
-        (None, None, 2, tokens, lanes), lambda s: (0, slots - 1 - s, 0, 0, at)
-    )
     return pl.pallas_call(
-        functools.partial(square_kernel, PARTS, TARGETS, repeat, heads, slots),
+        functools.partial(square_kernel, parts_of, targets, repeat, heads, slots),
         grid=(slots,),
         in_specs=[
             pl.BlockSpec(memory_space=pltpu.SMEM),
-            pl.BlockSpec(memory_space=pltpu.SMEM),
             head_block,
-            pl.BlockSpec((None, tokens, repeat * lanes), lambda s: (0, 0, at)),
+            pl.BlockSpec((tokens, repeat * lanes), lambda s: (0, 0)),
             head_block,
-            own_block,
         ]
-        + [pl.BlockSpec((None, 2, half, lanes), lambda s: (slots - 1 - s, 0, 0, 0))] * 6,
+        + [
+            pl.BlockSpec((None, 2, len(parts) * half, lanes), lambda s: (slots - 1 - s, 0, 0, 0))
+            for parts in parts_of
+        ],
         out_specs=[pl.BlockSpec((tokens, repeat * lanes), lambda s: (0, 0))]
         + [
             pl.BlockSpec((None, 2, len(parts) * half, lanes), lambda s: (slots - 1 - s, 0, 0, 0))
-            for parts in TARGETS
+            for parts in targets
         ],
         out_shape=[jax.ShapeDtypeStruct((tokens, repeat * lanes), jnp.bfloat16)]
         + [
             jax.ShapeDtypeStruct((slots, 2, len(parts) * half, lanes), dtype)
-            for parts, dtype in zip(TARGETS, TARGET_TYPES)
+            for parts, dtype in zip(targets, types)
         ],
         scratch_shapes=[
             pltpu.VMEM((tokens, repeat * lanes), jnp.bfloat16),
@@ -352,7 +346,7 @@
             transcendentals=slots * tokens * repeat * heads * keys_total,
         ),
         name=f"layers_{start}",
-    )(span_order, section_layers, queries, gradient, saved_out, *pieces)
+    )(meta, queries, gradient, saved_out, *pieces)
 
 
 CHUNKS = ((0, 2), (2, 4))
@@ -363,46 +357,63 @@
     if lax.axis_size("ctx") != 4 or keyvals.shape[4] != CHUNKS[-1][1] * DH:
         return general_device(queries, keyvals, saved_out, grad_in, section_layers, span_order)
 
-    def gathered(start, stop):
+    meta = jnp.concatenate([span_order, section_layers])
+
+    def block_of(chunk, after):
+        start, stop = chunk
         own = keyvals[0, :, :, :, start * DH : stop * DH]
+        if after:
+            own, _ = lax.optimization_barrier((own, after))
+        return own
+
+    def by_halves(own):
         low = own[:, :, :half]
         high = own[:, :, half:]
         x_high = exchanged(high, "ctx", 1)
+        x_low = exchanged(low, "ctx", 1)
         y_low = exchanged(low, "ctx", 2)
-        x_low = exchanged(low, "ctx", 1)
         y_high = exchanged(high, "ctx", 2)
+        far_high = exchanged(x_high, "ctx", 2)
         far_low = exchanged(y_low, "ctx", 1)
-        far_high = exchanged(x_high, "ctx", 2)
-        return [keyvals, x_low, x_high, y_low, y_high, far_low, far_high]
-
-    def reduced(mine, first_x, first_y, rest_x, rest_y):
+        return [own, x_low, x_high, y_low, y_high, far_low, far_high], HALVES
+
+    def direct(own):
+        return [own] + [exchanged(own, "ctx", mask) for mask in (1, 2, 3)], WHOLES
+
+    def two_phases(mine, first_x, first_y, rest_x, rest_y):
         got_x = exchanged(first_x, "ctx", 1)
         got_y = exchanged(first_y, "ctx", 2)
-        second_x = (rest_x + got_y[:, :, :half].astype(jnp.float32)).astype(jnp.bfloat16)
-        second_y = (rest_y + got_x[:, :, :half].astype(jnp.float32)).astype(jnp.bfloat16)
+        second_x = (rest_x + got_y[:, :, :half].astype(FLOAT)).astype(SHORT)
+        second_y = (rest_y + got_x[:, :, :half].astype(FLOAT)).astype(SHORT)
         more_x = exchanged(second_x, "ctx", 1)
         more_y = exchanged(second_y, "ctx", 2)
-        low = (
-            mine[:, :, :half]
-            + got_x[:, :, half:].astype(jnp.float32)
-            + more_y.astype(jnp.float32)
-        )
-        high = (
-            mine[:, :, half:]
-            + got_y[:, :, half:].astype(jnp.float32)
-            + more_x.astype(jnp.float32)
-        )
-        return jnp.concatenate([low, high], axis=2).astype(jnp.bfloat16)
-
-    pieces = [gathered(start, stop) for start, stop in CHUNKS]
+        low = mine[:, :, :half] + got_x[:, :, half:].astype(FLOAT) + more_y.astype(FLOAT)
+        high = mine[:, :, half:] + got_y[:, :, half:].astype(FLOAT) + more_x.astype(FLOAT)
+        return jnp.concatenate([low, high], axis=2).astype(SHORT)
+
+    gathers = [by_halves, direct]
+    pieces = []
+    for at, chunk in enumerate(CHUNKS):
+        after = []
+        if at == 1:
+            after = [pieces[0][0][i] for i in (2,)]
+        pieces.append(gathers[at](block_of(chunk, after)))
+    repeat = queries.shape[3] // keyvals.shape[4]
+
+    def columns(array, start, stop):
+        return array[..., start * repeat * DH : stop * repeat * DH]
+
     key_parts = []
     down_parts = []
-    for (start, stop), own_pieces in zip(CHUNKS, pieces):
+    results = []
+    for (start, stop), (own_pieces, parts_of), how in zip(CHUNKS, pieces, [(TWO_PHASES, (FLOAT, SHORT, SHORT, FLOAT, FLOAT), two_phases), (TWO_PHASES, (FLOAT, SHORT, SHORT, FLOAT, FLOAT), two_phases)]):
+        targets, types, join = how
         gradient, *parts = square_layers(
-            start, stop - start, span_order, section_layers, queries, grad_in, saved_out, own_pieces
+            start, stop - start, meta, queries, columns(grad_in[0], start, stop), saved_out, own_pieces, parts_of, targets, types
         )
-        down_parts.append(shifted(gradient, "section", -1))
-        key_parts.append(reduced(*parts))
+        results.append(gradient)
+        key_parts.append(join(*parts))
+    down_parts = [shifted(result, "section", -1) for result in results]
     grad_kv = jnp.concatenate(key_parts, axis=3)[None]
     grad_down = jnp.concatenate(down_parts, axis=1)[None]
     return (grad_kv, grad_down)

time: 55.8 us -> 54.3 us (0.973); the launches traced: 55 us -> 54.1 us
  starting transfers between devices: 33.6 us -> 22.5 us
  waiting for transfers between devices: 8.32 us -> 14 us
  Pallas kernels: 8.82 us -> 13.2 us
    ppermute x2, starting transfers between devices: 8.01 us -> 0.44 us  [shifted(): lax.ppermute(array, axis, [(i, (i + by) % length) for i in range(length)])]
    ppermute x20 -> x17, waiting for transfers between devices: 8.32 us -> 14 us  [exchanged(): return lax.ppermute(array, axis, [(i, i ^ mask) for i in range(length)])]
    pallas_call x2, Pallas kernels: 8.82 us -> 13.2 us  [square_layers(): pl.pallas_call(functools.partial(square_kernel, parts_of, targets, repeat...]
    ppermute x20 -> x17, starting transfers between devices: 25.6 us -> 22 us  [exchanged(): return lax.ppermute(array, axis, [(i, i ^ mask) for i in range(length)])]
  transfers between devices with their start and end apart: 22 -> 19, of which waited for: 7 -> 10; matrix products, arithmetic and copies ran while one was open for 2% -> 2% of each run, Pallas kernels for 16% -> 24%
where the time goes in v3:
time: 54.3 us; the launch traced here: 54.1 us
  starting transfers between devices  22.5 us (41%)
  waiting for transfers between devices  14 us (26%)
  Pallas kernels  13.2 us (24%)
  other arithmetic  2.28 us (4%)
  local copies, waits for them, and re-layouts  1.35 us (2%)
  between operations  0.76 us (1%)
    ppermute x17, starting transfers between devices, exchanged(): return lax.ppermute(array, axis, [(i, i ^ mask) for i in range(length)])  22 us
    ppermute x17, waiting for transfers between devices, exchanged(): return lax.ppermute(array, axis, [(i, i ^ mask) for i in range(length)])  14 us
    pallas_call x2, Pallas kernels, square_layers(): pl.pallas_call(functools.partial(square_kernel, parts_of, targets, repeat...  13.2 us
    squeeze x1, local copies, waits for them, and re-layouts, block_of(): own = keyvals[0, :, :, :, start * DH:stop * DH]  1.22 us
  transfers between devices with their start and end apart: 19, of which 10 were waited for; matrix products, arithmetic and copies ran while one was open for 2% of the time, Pallas kernels for 24%

profile of v3, /device:TPU:0, one launch (start us, length us, event | category | flops | bytes accessed | tf_op | source)
XLA Modules:
  0.0 54.1 jit_solution(3714125732425369191)
XLA Ops:
  0.6 0.0 copy-start.1
  0.7 1.2 %slice_bitcast_fusion.1 = (bf16[2,2,128,256]{3,2,1,0:T(8,128)(2,1)S(1)}, bf16[2,2,128,256]{3,2,1,0:T(8,128)(2,1)S(1)}) fusion(bf16[1,2,2,128,512]{4,3,2,1,0:T(8,128)(2,1)} %param.7), kind=kLoop, calls=%fused_computation.11 | loop fusion | bytes 1048576 | tf_op jit(solution)/shard_map/squeeze | solution.py:364
  1.9 3.0 %collective-permute-start.2 = (bf16[2,2,64,256]{3,2,1,0:T(8,128)(2,1)S(1)}, bf16[2,2,64,256]{3,2,1,0:T(8,128)(2,1)S(1)}, u32[]{:S(2)}, u32[]{:S(2)}) collective-permute-start(bf16[2,2,64,256]{3,2,1,0:T(8,128)(2,1)S(1)} %get-tuple-element.36), channel_id=1, source_target_pairs={{0,2},{1,3},{2,0},{3,1},{4,6},{5,7},{6,4},{7,5},{8,10},{9,11},{10,... | collective-permute-start | bytes 393224 | tf_op jit(solution)/shard_map/ppermute | solution.py:18
  5.0 1.5 %collective-permute-start.1 = (bf16[2,2,64,256]{3,2,1,0:T(8,128)(2,1)S(1)}, bf16[2,2,64,256]{3,2,1,0:T(8,128)(2,1)S(1)}, u32[]{:S(2)}, u32[]{:S(2)}) collective-permute-start(bf16[2,2,64,256]{3,2,1,0:T(8,128)(2,1)S(1)} %get-tuple-element.37), channel_id=1, source_target_pairs={{0,1},{1,0},{2,3},{3,2},{4,5},{5,4},{6,7},{7,6},{8,9},{9,8},{10,11... | collective-permute-start | bytes 393224 | tf_op jit(solution)/shard_map/ppermute | solution.py:18
  6.4 0.5 collective-permute-start
  7.0 0.1 collective-permute-start.3
  7.1 1.8 %collective-permute-done.2.refs_3_ = bf16[2,2,64,256]{3,2,1,0:T(8,128)(2,1)S(1)} collective-permute-done((bf16[2,2,64,256]{3,2,1,0:T(8,128)(2,1)S(1)}, bf16[2,2,64,256]{3,2,1,0:T(8,128)(2,1)S(1)}, u32[]{:S(2)}, u32[]{:S(2)}) %collective-permute-start.2) | collective-permute-done | bytes 131104 | tf_op jit(solution)/shard_map/ppermute | solution.py:18
  8.9 1.5 %collective-permute-start.4 = (bf16[2,2,64,256]{3,2,1,0:T(8,128)(2,1)S(1)}, bf16[2,2,64,256]{3,2,1,0:T(8,128)(2,1)S(1)}, u32[]{:S(2)}, u32[]{:S(2)}) collective-permute-start(bf16[2,2,64,256]{3,2,1,0:T(8,128)(2,1)S(1)} %collective-permute-done.2.refs_3_), channel_id=1, source_target_pairs={{0,1},{1,0},{2,3},{3,2},{4,5},{5,4},{6,7},{7,6},{8,9},{9,8},{10,11... | collective-permute-start | bytes 393224 | tf_op jit(solution)/shard_map/ppermute | solution.py:18
  10.3 1.1 %collective-permute-done.1.refs_2_ = bf16[2,2,64,256]{3,2,1,0:T(8,128)(2,1)S(1)} collective-permute-done((bf16[2,2,64,256]{3,2,1,0:T(8,128)(2,1)S(1)}, bf16[2,2,64,256]{3,2,1,0:T(8,128)(2,1)S(1)}, u32[]{:S(2)}, u32[]{:S(2)}) %collective-permute-start.1) | collective-permute-done | bytes 131104 | tf_op jit(solution)/shard_map/ppermute | solution.py:18
  11.4 1.4 %collective-permute-start.5 = (bf16[2,2,64,256]{3,2,1,0:T(8,128)(2,1)S(1)}, bf16[2,2,64,256]{3,2,1,0:T(8,128)(2,1)S(1)}, u32[]{:S(2)}, u32[]{:S(2)}) collective-permute-start(bf16[2,2,64,256]{3,2,1,0:T(8,128)(2,1)S(1)} %collective-permute-done.1.refs_2_), channel_id=1, source_target_pairs={{0,2},{1,3},{2,0},{3,1},{4,6},{5,7},{6,4},{7,5},{8,10},{9,11},{10,... | collective-permute-start | bytes 393224 | tf_op jit(solution)/shard_map/ppermute | solution.py:18
  12.8 0.1 fusion
  12.9 0.1 pad_add_fusion.meta_ref
  13.0 0.6 %collective-permute-start.10 = (bf16[2,2,128,256]{3,2,1,0:T(8,128)(2,1)S(1)}, bf16[2,2,128,256]{3,2,1,0:T(8,128)(2,1)S(1)}, u32[]{:S(2)}, u32[]{:S(2)}) collective-permute-start(bf16[2,2,128,256]{3,2,1,0:T(8,128)(2,1)S(1)} %get-tuple-element.20.refs_0_), channel_id=1, source_target_pairs={{0,1},{1,0},{2,3},{3,2},{4,5},{5,4},{6,7},{7,6},{8,9},{9,8},{10,11... | collective-permute-start | bytes 786440 | tf_op jit(solution)/shard_map/ppermute | solution.py:18
  13.6 0.6 %collective-permute-done.refs_1_ = bf16[2,2,64,256]{3,2,1,0:T(8,128)(2,1)S(1)} collective-permute-done((bf16[2,2,64,256]{3,2,1,0:T(8,128)(2,1)S(1)}, bf16[2,2,64,256]{3,2,1,0:T(8,128)(2,1)S(1)}, u32[]{:S(2)}, u32[]{:S(2)}) %collective-permute-start) | collective-permute-done | bytes 131104 | tf_op jit(solution)/shard_map/ppermute | solution.py:18
  14.2 0.9 %collective-permute-start.11 = (bf16[2,2,128,256]{3,2,1,0:T(8,128)(2,1)S(1)}, bf16[2,2,128,256]{3,2,1,0:T(8,128)(2,1)S(1)}, u32[]{:S(2)}, u32[]{:S(2)}) collective-permute-start(bf16[2,2,128,256]{3,2,1,0:T(8,128)(2,1)S(1)} %get-tuple-element.20.refs_0_), channel_id=1, source_target_pairs={{0,2},{1,3},{2,0},{3,1},{4,6},{5,7},{6,4},{7,5},{8,10},{9,11},{10,... | collective-permute-start | bytes 786440 | tf_op jit(solution)/shard_map/ppermute | solution.py:18
  15.1 0.0 collective-permute-done.3.refs_4_
  15.1 2.0 %collective-permute-start.12 = (bf16[2,2,128,256]{3,2,1,0:T(8,128)(2,1)S(1)}, bf16[2,2,128,256]{3,2,1,0:T(8,128)(2,1)S(1)}, u32[]{:S(2)}, u32[]{:S(2)}) collective-permute-start(bf16[2,2,128,256]{3,2,1,0:T(8,128)(2,1)S(1)} %get-tuple-element.20.refs_0_), channel_id=1, source_target_pairs={{0,3},{1,2},{2,1},{3,0},{4,7},{5,6},{6,5},{7,4},{8,11},{9,10},{10,... | collective-permute-start | bytes 786440 | tf_op jit(solution)/shard_map/ppermute | solution.py:18
  17.1 0.0 collective-permute-done.4.refs_5_
  17.1 0.6 %collective-permute-done.5.refs_6_ = bf16[2,2,64,256]{3,2,1,0:T(8,128)(2,1)S(1)} collective-permute-done((bf16[2,2,64,256]{3,2,1,0:T(8,128)(2,1)S(1)}, bf16[2,2,64,256]{3,2,1,0:T(8,128)(2,1)S(1)}, u32[]{:S(2)}, u32[]{:S(2)}) %collective-permute-start.5) | collective-permute-done | bytes 131104 | tf_op jit(solution)/shard_map/ppermute | solution.py:18
  17.7 6.6 %layers_0.1 = (bf16[128,2048]{1,0:T(8,128)(2,1)S(1)}, f32[2,2,128,256]{3,2,1,0:T(8,128)S(1)}, bf16[2,2,128,256]{3,2,1,0:T(8,128)(2,1)S(1)}, bf16[2,2,128,256]{3,...) custom-call(s32[16]{0:T(128)S(1)} %pad_add_fusion.meta_ref, ...), custom_call_target="tpu_custom_call" | custom-call | flops 2684354560 | bytes 8388608 | tf_op jit(solution)/shard_map/layers_0/pallas_call | solution.py:308
  24.4 1.4 %collective-permute-start.6 = (bf16[2,2,128,256]{3,2,1,0:T(8,128)(2,1)S(1)}, bf16[2,2,128,256]{3,2,1,0:T(8,128)(2,1)S(1)}, u32[]{:S(2)}, u32[]{:S(2)}) collective-permute-start(bf16[2,2,128,256]{3,2,1,0:T(8,128)(2,1)S(1)} %get-tuple-element.16), channel_id=1, source_target_pairs={{0,1},{1,0},{2,3},{3,2},{4,5},{5,4},{6,7},{7,6},{8,9},{9,8},{10,11... | collective-permute-start | bytes 786440 | tf_op jit(solution)/shard_map/ppermute | solution.py:18
  25.8 0.6 %collective-permute-start.8 = (bf16[2,2,128,256]{3,2,1,0:T(8,128)(2,1)S(1)}, bf16[2,2,128,256]{3,2,1,0:T(8,128)(2,1)S(1)}, u32[]{:S(2)}, u32[]{:S(2)}) collective-permute-start(bf16[2,2,128,256]{3,2,1,0:T(8,128)(2,1)S(1)} %get-tuple-element.18), channel_id=1, source_target_pairs={{0,2},{1,3},{2,0},{3,1},{4,6},{5,7},{6,4},{7,5},{8,10},{9,11},{10,... | collective-permute-start | bytes 786440 | tf_op jit(solution)/shard_map/ppermute | solution.py:18
  26.4 0.0 collective-permute-done.10.refs_1_
  26.4 0.0 collective-permute-start.17
  26.4 0.0 collective-permute-done.11.refs_2_
  26.4 2.1 %collective-permute-done.12.refs_3_ = bf16[2,2,128,256]{3,2,1,0:T(8,128)(2,1)S(1)} collective-permute-done((bf16[2,2,128,256]{3,2,1,0:T(8,128)(2,1)S(1)}, bf16[2,2,128,256]{3,2,1,0:T(8,128)(2,1)S(1)}, u32[]{:S(2)}, u32[]{:S(2)}) %collective-permute-start.12) | collective-permute-done | bytes 262176 | tf_op jit(solution)/shard_map/ppermute | solution.py:18
  28.5 6.6 %layers_2.1 = (bf16[128,2048]{1,0:T(8,128)(2,1)S(1)}, f32[2,2,128,256]{3,2,1,0:T(8,128)S(1)}, bf16[2,2,128,256]{3,2,1,0:T(8,128)(2,1)S(1)}, bf16[2,2,128,256]{3,...) custom-call(s32[16]{0:T(128)S(1)} %pad_add_fusion.meta_ref, ...), custom_call_target="tpu_custom_call" | custom-call | flops 2684354560 | bytes 8388608 | tf_op jit(solution)/shard_map/layers_2/pallas_call | solution.py:308
  35.1 1.4 %collective-permute-start.13 = (bf16[2,2,128,256]{3,2,1,0:T(8,128)(2,1)S(1)}, bf16[2,2,128,256]{3,2,1,0:T(8,128)(2,1)S(1)}, u32[]{:S(2)}, u32[]{:S(2)}) collective-permute-start(bf16[2,2,128,256]{3,2,1,0:T(8,128)(2,1)S(1)} %get-tuple-element.22), channel_id=1, source_target_pairs={{0,1},{1,0},{2,3},{3,2},{4,5},{5,4},{6,7},{7,6},{8,9},{9,8},{10,11... | collective-permute-start | bytes 786440 | tf_op jit(solution)/shard_map/ppermute | solution.py:18
  36.5 1.3 %collective-permute-start.15 = (bf16[2,2,128,256]{3,2,1,0:T(8,128)(2,1)S(1)}, bf16[2,2,128,256]{3,2,1,0:T(8,128)(2,1)S(1)}, u32[]{:S(2)}, u32[]{:S(2)}) collective-permute-start(bf16[2,2,128,256]{3,2,1,0:T(8,128)(2,1)S(1)} %get-tuple-element.24), channel_id=1, source_target_pairs={{0,2},{1,3},{2,0},{3,1},{4,6},{5,7},{6,4},{7,5},{8,10},{9,11},{10,... | collective-permute-start | bytes 786440 | tf_op jit(solution)/shard_map/ppermute | solution.py:18
  37.9 0.0 collective-permute-done.6
  37.9 0.4 collective-permute-start.18
  38.3 0.0 collective-permute-done.8
  38.4 1.1 %collective-permute-start.7 = (bf16[2,2,64,256]{3,2,1,0:T(8,128)(2,1)S(1)}, bf16[2,2,64,256]{3,2,1,0:T(8,128)(2,1)S(1)}, u32[]{:S(2)}, u32[]{:S(2)}) collective-permute-start(bf16[2,2,64,256]{3,2,1,0:T(8,128)(2,1)S(1)} %add_convert_fusion.7), channel_id=1, source_target_pairs={{0,2},{1,3},{2,0},{3,1},{4,6},{5,7},{6,4},{7,5},{8,10},{9,11},{10,... | collective-permute-start | bytes 393224 | tf_op jit(solution)/shard_map/ppermute | solution.py:18
  39.5 2.1 %collective-permute-done.13 = bf16[2,2,128,256]{3,2,1,0:T(8,128)(2,1)S(1)} collective-permute-done((bf16[2,2,128,256]{3,2,1,0:T(8,128)(2,1)S(1)}, bf16[2,2,128,256]{3,2,1,0:T(8,128)(2,1)S(1)}, u32[]{:S(2)}, u32[]{:S(2)}) %collective-permute-start.13) | collective-permute-done | bytes 262176 | tf_op jit(solution)/shard_map/ppermute | solution.py:18
  41.5 1.9 %collective-permute-start.9 = (bf16[2,2,64,256]{3,2,1,0:T(8,128)(2,1)S(1)}, bf16[2,2,64,256]{3,2,1,0:T(8,128)(2,1)S(1)}, u32[]{:S(2)}, u32[]{:S(2)}) collective-permute-start(bf16[2,2,64,256]{3,2,1,0:T(8,128)(2,1)S(1)} %add_convert_fusion.5), channel_id=1, source_target_pairs={{0,1},{1,0},{2,3},{3,2},{4,5},{5,4},{6,7},{7,6},{8,9},{9,8},{10,11... | collective-permute-start | bytes 393224 | tf_op jit(solution)/shard_map/ppermute | solution.py:18
  43.5 1.2 %collective-permute-done.15 = bf16[2,2,128,256]{3,2,1,0:T(8,128)(2,1)S(1)} collective-permute-done((bf16[2,2,128,256]{3,2,1,0:T(8,128)(2,1)S(1)}, bf16[2,2,128,256]{3,2,1,0:T(8,128)(2,1)S(1)}, u32[]{:S(2)}, u32[]{:S(2)}) %collective-permute-start.15) | collective-permute-done | bytes 262176 | tf_op jit(solution)/shard_map/ppermute | solution.py:18
  44.7 2.0 %collective-permute-start.14 = (bf16[2,2,64,256]{3,2,1,0:T(8,128)(2,1)S(1)}, bf16[2,2,64,256]{3,2,1,0:T(8,128)(2,1)S(1)}, u32[]{:S(2)}, u32[]{:S(2)}) collective-permute-start(bf16[2,2,64,256]{3,2,1,0:T(8,128)(2,1)S(1)} %add_convert_fusion.3), channel_id=1, source_target_pairs={{0,2},{1,3},{2,0},{3,1},{4,6},{5,7},{6,4},{7,5},{8,10},{9,11},{10,... | collective-permute-start | bytes 393224 | tf_op jit(solution)/shard_map/ppermute | solution.py:18
  46.8 0.4 collective-permute-done.7
  47.1 0.7 %collective-permute-start.16 = (bf16[2,2,64,256]{3,2,1,0:T(8,128)(2,1)S(1)}, bf16[2,2,64,256]{3,2,1,0:T(8,128)(2,1)S(1)}, u32[]{:S(2)}, u32[]{:S(2)}) collective-permute-start(bf16[2,2,64,256]{3,2,1,0:T(8,128)(2,1)S(1)} %add_convert_fusion.1), channel_id=1, source_target_pairs={{0,1},{1,0},{2,3},{3,2},{4,5},{5,4},{6,7},{7,6},{8,9},{9,8},{10,11... | collective-permute-start | bytes 393224 | tf_op jit(solution)/shard_map/ppermute | solution.py:18
  47.8 0.0 collective-permute-done.9
  47.8 0.1 add_convert_fusion.6
  47.9 1.8 %collective-permute-done.14 = bf16[2,2,64,256]{3,2,1,0:T(8,128)(2,1)S(1)} collective-permute-done((bf16[2,2,64,256]{3,2,1,0:T(8,128)(2,1)S(1)}, bf16[2,2,64,256]{3,2,1,0:T(8,128)(2,1)S(1)}, u32[]{:S(2)}, u32[]{:S(2)}) %collective-permute-start.14) | collective-permute-done | bytes 131104 | tf_op jit(solution)/shard_map/ppermute | solution.py:18
  49.7 2.4 %collective-permute-done.16 = bf16[2,2,64,256]{3,2,1,0:T(8,128)(2,1)S(1)} collective-permute-done((bf16[2,2,64,256]{3,2,1,0:T(8,128)(2,1)S(1)}, bf16[2,2,64,256]{3,2,1,0:T(8,128)(2,1)S(1)}, u32[]{:S(2)}, u32[]{:S(2)}) %collective-permute-start.16) | collective-permute-done | bytes 131104 | tf_op jit(solution)/shard_map/ppermute | solution.py:18
  52.1 0.1 add_convert_fusion.2
  52.2 0.8 %maximum_bitcast_fusion.1 = bf16[1,2,2,128,512]{4,3,2,1,0:T(8,128)(2,1)} fusion(bf16[2,2,64,256]{3,2,1,0:T(8,128)(2,1)S(1)} %get-tuple-element.33, bf16[2,2,64,256]{3,2,1,0:T(8,128)(2,1)S(1)} %get-tuple-element.32, bf16[2,2,64,256]{3,2,1,0:T(8,128)(2,1)S(1)} %get-tuple-element.31, bf16[2,2,64,256]{3,2,1,0:T(8,128)(2,1)S(1)} %get-tuple-element.30), kind=kLoop, calls=%fused_computation.1 | loop fusion | flops 2097152 | bytes 1048576 | tf_op jit(solution)/shard_map/broadcast_in_dim | solution.py:417
  53.0 0.0 collective-permute-done.17
  53.0 0.0 collective-permute-done.18
  53.0 1.1 %maximum_bitcast_fusion = bf16[1,128,4096]{2,1,0:T(8,128)(2,1)} fusion(bf16[128,2048]{1,0:T(8,128)(2,1)S(1)} %collective-permute-done.18, bf16[128,2048]{1,0:T(8,128)(2,1)S(1)} %collective-permute-done.17), kind=kLoop, calls=%fused_computation | loop fusion | flops 2097152 | bytes 2097152 | tf_op jit(solution)/shard_map/broadcast_in_dim | solution.py:418
  (12 shorter events, 0.2 us)
Async XLA Ops:
  0.6 12.2 %copy-start.1 = (bf16[1,128,4096]{2,1,0:T(8,128)(2,1)S(1)}, bf16[1,128,4096]{2,1,0:T(8,128)(2,1)}, u32[]{:S(2)}) copy-start(bf16[1,128,4096]{2,1,0:T(8,128)(2,1)} %param.9) | copy-start | bytes 3145732
  0.6 12.3 %copy-start.2 = (s32[8]{0:T(128)S(1)}, s32[8]{0:T(128)}, u32[]{:S(2)}) copy-start(s32[8]{0:T(128)} %param.10) | copy-start | bytes 100
  0.7 12.3 %copy-start.3 = (s32[8]{0:T(128)S(1)}, s32[8]{0:T(128)}, u32[]{:S(2)}) copy-start(s32[8]{0:T(128)} %param.11) | copy-start | bytes 100
  0.7 17.1 %copy-start = (bf16[1,2,128,4096]{3,2,1,0:T(8,128)(2,1)S(1)}, bf16[1,2,128,4096]{3,2,1,0:T(8,128)(2,1)}, u32[]{:S(2)}) copy-start(bf16[1,2,128,4096]{3,2,1,0:T(8,128)(2,1)} %q_ref.3) | copy-start | bytes 6291460
  1.9 6.9 %collective-permute-start.2 = (bf16[2,2,64,256]{3,2,1,0:T(8,128)(2,1)S(1)}, bf16[2,2,64,256]{3,2,1,0:T(8,128)(2,1)S(1)}, u32[]{:S(2)}, u32[]{:S(2)}) collective-permute-start(bf16[2,2,64,256]{3,2,1,0:T(8,128)(2,1)S(1)} %get-tuple-element.36), channel_id=1, source_target_pairs={{0,2},{1,3},{2,0},{3,1},{4,6},{5,7},{6,4},{7,5},{8,10},{9,11},{10,... | collective-permute-start | bytes 393224 | tf_op jit(solution)/shard_map/ppermute | solution.py:18
  5.0 6.4 %collective-permute-start.1 = (bf16[2,2,64,256]{3,2,1,0:T(8,128)(2,1)S(1)}, bf16[2,2,64,256]{3,2,1,0:T(8,128)(2,1)S(1)}, u32[]{:S(2)}, u32[]{:S(2)}) collective-permute-start(bf16[2,2,64,256]{3,2,1,0:T(8,128)(2,1)S(1)} %get-tuple-element.37), channel_id=1, source_target_pairs={{0,1},{1,0},{2,3},{3,2},{4,5},{5,4},{6,7},{7,6},{8,9},{9,8},{10,11... | collective-permute-start | bytes 393224 | tf_op jit(solution)/shard_map/ppermute | solution.py:18
  6.4 7.7 %collective-permute-start = (bf16[2,2,64,256]{3,2,1,0:T(8,128)(2,1)S(1)}, bf16[2,2,64,256]{3,2,1,0:T(8,128)(2,1)S(1)}, u32[]{:S(2)}, u32[]{:S(2)}) collective-permute-start(bf16[2,2,64,256]{3,2,1,0:T(8,128)(2,1)S(1)} %get-tuple-element.36), channel_id=1, source_target_pairs={{0,1},{1,0},{2,3},{3,2},{4,5},{5,4},{6,7},{7,6},{8,9},{9,8},{10,11... | collective-permute-start | bytes 393224 | tf_op jit(solution)/shard_map/ppermute | solution.py:18
  7.0 8.1 %collective-permute-start.3 = (bf16[2,2,64,256]{3,2,1,0:T(8,128)(2,1)S(1)}, bf16[2,2,64,256]{3,2,1,0:T(8,128)(2,1)S(1)}, u32[]{:S(2)}, u32[]{:S(2)}) collective-permute-start(bf16[2,2,64,256]{3,2,1,0:T(8,128)(2,1)S(1)} %get-tuple-element.37), channel_id=1, source_target_pairs={{0,2},{1,3},{2,0},{3,1},{4,6},{5,7},{6,4},{7,5},{8,10},{9,11},{10,... | collective-permute-start | bytes 393224 | tf_op jit(solution)/shard_map/ppermute | solution.py:18
  8.9 8.3 %collective-permute-start.4 = (bf16[2,2,64,256]{3,2,1,0:T(8,128)(2,1)S(1)}, bf16[2,2,64,256]{3,2,1,0:T(8,128)(2,1)S(1)}, u32[]{:S(2)}, u32[]{:S(2)}) collective-permute-start(bf16[2,2,64,256]{3,2,1,0:T(8,128)(2,1)S(1)} %collective-permute-done.2.refs_3_), channel_id=1, source_target_pairs={{0,1},{1,0},{2,3},{3,2},{4,5},{5,4},{6,7},{7,6},{8,9},{9,8},{10,11... | collective-permute-start | bytes 393224 | tf_op jit(solution)/shard_map/ppermute | solution.py:18
  11.4 6.4 %collective-permute-start.5 = (bf16[2,2,64,256]{3,2,1,0:T(8,128)(2,1)S(1)}, bf16[2,2,64,256]{3,2,1,0:T(8,128)(2,1)S(1)}, u32[]{:S(2)}, u32[]{:S(2)}) collective-permute-start(bf16[2,2,64,256]{3,2,1,0:T(8,128)(2,1)S(1)} %collective-permute-done.1.refs_2_), channel_id=1, source_target_pairs={{0,2},{1,3},{2,0},{3,1},{4,6},{5,7},{6,4},{7,5},{8,10},{9,11},{10,... | collective-permute-start | bytes 393224 | tf_op jit(solution)/shard_map/ppermute | solution.py:18
  13.0 13.4 %collective-permute-start.10 = (bf16[2,2,128,256]{3,2,1,0:T(8,128)(2,1)S(1)}, bf16[2,2,128,256]{3,2,1,0:T(8,128)(2,1)S(1)}, u32[]{:S(2)}, u32[]{:S(2)}) collective-permute-start(bf16[2,2,128,256]{3,2,1,0:T(8,128)(2,1)S(1)} %get-tuple-element.20.refs_0_), channel_id=1, source_target_pairs={{0,1},{1,0},{2,3},{3,2},{4,5},{5,4},{6,7},{7,6},{8,9},{9,8},{10,11... | collective-permute-start | bytes 786440 | tf_op jit(solution)/shard_map/ppermute | solution.py:18
  14.2 12.2 %collective-permute-start.11 = (bf16[2,2,128,256]{3,2,1,0:T(8,128)(2,1)S(1)}, bf16[2,2,128,256]{3,2,1,0:T(8,128)(2,1)S(1)}, u32[]{:S(2)}, u32[]{:S(2)}) collective-permute-start(bf16[2,2,128,256]{3,2,1,0:T(8,128)(2,1)S(1)} %get-tuple-element.20.refs_0_), channel_id=1, source_target_pairs={{0,2},{1,3},{2,0},{3,1},{4,6},{5,7},{6,4},{7,5},{8,10},{9,11},{10,... | collective-permute-start | bytes 786440 | tf_op jit(solution)/shard_map/ppermute | solution.py:18
  15.1 13.4 %collective-permute-start.12 = (bf16[2,2,128,256]{3,2,1,0:T(8,128)(2,1)S(1)}, bf16[2,2,128,256]{3,2,1,0:T(8,128)(2,1)S(1)}, u32[]{:S(2)}, u32[]{:S(2)}) collective-permute-start(bf16[2,2,128,256]{3,2,1,0:T(8,128)(2,1)S(1)} %get-tuple-element.20.refs_0_), channel_id=1, source_target_pairs={{0,3},{1,2},{2,1},{3,0},{4,7},{5,6},{6,5},{7,4},{8,11},{9,10},{10,... | collective-permute-start | bytes 786440 | tf_op jit(solution)/shard_map/ppermute | solution.py:18
  24.4 13.5 %collective-permute-start.6 = (bf16[2,2,128,256]{3,2,1,0:T(8,128)(2,1)S(1)}, bf16[2,2,128,256]{3,2,1,0:T(8,128)(2,1)S(1)}, u32[]{:S(2)}, u32[]{:S(2)}) collective-permute-start(bf16[2,2,128,256]{3,2,1,0:T(8,128)(2,1)S(1)} %get-tuple-element.16), channel_id=1, source_target_pairs={{0,1},{1,0},{2,3},{3,2},{4,5},{5,4},{6,7},{7,6},{8,9},{9,8},{10,11... | collective-permute-start | bytes 786440 | tf_op jit(solution)/shard_map/ppermute | solution.py:18
  25.8 12.5 %collective-permute-start.8 = (bf16[2,2,128,256]{3,2,1,0:T(8,128)(2,1)S(1)}, bf16[2,2,128,256]{3,2,1,0:T(8,128)(2,1)S(1)}, u32[]{:S(2)}, u32[]{:S(2)}) collective-permute-start(bf16[2,2,128,256]{3,2,1,0:T(8,128)(2,1)S(1)} %get-tuple-element.18), channel_id=1, source_target_pairs={{0,2},{1,3},{2,0},{3,1},{4,6},{5,7},{6,4},{7,5},{8,10},{9,11},{10,... | collective-permute-start | bytes 786440 | tf_op jit(solution)/shard_map/ppermute | solution.py:18
  26.4 26.6 %collective-permute-start.17 = (bf16[128,2048]{1,0:T(8,128)(2,1)S(1)}, bf16[128,2048]{1,0:T(8,128)(2,1)S(1)}, u32[]{:S(2)}, u32[]{:S(2)}) collective-permute-start(bf16[128,2048]{1,0:T(8,128)(2,1)S(1)} %get-tuple-element.26), channel_id=1, source_target_pairs={{0,28},{4,0},{8,4},{12,8},{16,12},{20,16},{24,20},{28,24},{1,29},{... | collective-permute-start | bytes 1572872 | tf_op jit(solution)/shard_map/ppermute | solution.py:23
  35.1 6.4 %collective-permute-start.13 = (bf16[2,2,128,256]{3,2,1,0:T(8,128)(2,1)S(1)}, bf16[2,2,128,256]{3,2,1,0:T(8,128)(2,1)S(1)}, u32[]{:S(2)}, u32[]{:S(2)}) collective-permute-start(bf16[2,2,128,256]{3,2,1,0:T(8,128)(2,1)S(1)} %get-tuple-element.22), channel_id=1, source_target_pairs={{0,1},{1,0},{2,3},{3,2},{4,5},{5,4},{6,7},{7,6},{8,9},{9,8},{10,11... | collective-permute-start | bytes 786440 | tf_op jit(solution)/shard_map/ppermute | solution.py:18
  36.5 8.2 %collective-permute-start.15 = (bf16[2,2,128,256]{3,2,1,0:T(8,128)(2,1)S(1)}, bf16[2,2,128,256]{3,2,1,0:T(8,128)(2,1)S(1)}, u32[]{:S(2)}, u32[]{:S(2)}) collective-permute-start(bf16[2,2,128,256]{3,2,1,0:T(8,128)(2,1)S(1)} %get-tuple-element.24), channel_id=1, source_target_pairs={{0,2},{1,3},{2,0},{3,1},{4,6},{5,7},{6,4},{7,5},{8,10},{9,11},{10,... | collective-permute-start | bytes 786440 | tf_op jit(solution)/shard_map/ppermute | solution.py:18
  37.9 15.2 %collective-permute-start.18 = (bf16[128,2048]{1,0:T(8,128)(2,1)S(1)}, bf16[128,2048]{1,0:T(8,128)(2,1)S(1)}, u32[]{:S(2)}, u32[]{:S(2)}) collective-permute-start(bf16[128,2048]{1,0:T(8,128)(2,1)S(1)} %get-tuple-element.27), channel_id=1, source_target_pairs={{0,28},{4,0},{8,4},{12,8},{16,12},{20,16},{24,20},{28,24},{1,29},{... | collective-permute-start | bytes 1572872 | tf_op jit(solution)/shard_map/ppermute | solution.py:23
  38.4 8.8 %collective-permute-start.7 = (bf16[2,2,64,256]{3,2,1,0:T(8,128)(2,1)S(1)}, bf16[2,2,64,256]{3,2,1,0:T(8,128)(2,1)S(1)}, u32[]{:S(2)}, u32[]{:S(2)}) collective-permute-start(bf16[2,2,64,256]{3,2,1,0:T(8,128)(2,1)S(1)} %add_convert_fusion.7), channel_id=1, source_target_pairs={{0,2},{1,3},{2,0},{3,1},{4,6},{5,7},{6,4},{7,5},{8,10},{9,11},{10,... | collective-permute-start | bytes 393224 | tf_op jit(solution)/shard_map/ppermute | solution.py:18
  41.5 6.2 %collective-permute-start.9 = (bf16[2,2,64,256]{3,2,1,0:T(8,128)(2,1)S(1)}, bf16[2,2,64,256]{3,2,1,0:T(8,128)(2,1)S(1)}, u32[]{:S(2)}, u32[]{:S(2)}) collective-permute-start(bf16[2,2,64,256]{3,2,1,0:T(8,128)(2,1)S(1)} %add_convert_fusion.5), channel_id=1, source_target_pairs={{0,1},{1,0},{2,3},{3,2},{4,5},{5,4},{6,7},{7,6},{8,9},{9,8},{10,11... | collective-permute-start | bytes 393224 | tf_op jit(solution)/shard_map/ppermute | solution.py:18
  44.7 5.0 %collective-permute-start.14 = (bf16[2,2,64,256]{3,2,1,0:T(8,128)(2,1)S(1)}, bf16[2,2,64,256]{3,2,1,0:T(8,128)(2,1)S(1)}, u32[]{:S(2)}, u32[]{:S(2)}) collective-permute-start(bf16[2,2,64,256]{3,2,1,0:T(8,128)(2,1)S(1)} %add_convert_fusion.3), channel_id=1, source_target_pairs={{0,2},{1,3},{2,0},{3,1},{4,6},{5,7},{6,4},{7,5},{8,10},{9,11},{10,... | collective-permute-start | bytes 393224 | tf_op jit(solution)/shard_map/ppermute | solution.py:18
  47.1 5.0 %collective-permute-start.16 = (bf16[2,2,64,256]{3,2,1,0:T(8,128)(2,1)S(1)}, bf16[2,2,64,256]{3,2,1,0:T(8,128)(2,1)S(1)}, u32[]{:S(2)}, u32[]{:S(2)}) collective-permute-start(bf16[2,2,64,256]{3,2,1,0:T(8,128)(2,1)S(1)} %add_convert_fusion.1), channel_id=1, source_target_pairs={{0,1},{1,0},{2,3},{3,2},{4,5},{5,4},{6,7},{7,6},{8,9},{9,8},{10,11... | collective-permute-start | bytes 393224 | tf_op jit(solution)/shard_map/ppermute | solution.py:18
